TPU v7x, 256 devices: a whole 4x4x8 slice. The times are simulated.
256 devices in a mesh: seq: 16 (over x, y), dp: 16 (over z, core).
Axes of the slice: x: 4, y: 4, z: 8, core: 2. Of those that a mesh axis runs over, the one named last changes fastest.
Arguments:
- query_rows: bfloat16 [16, 4096, 2048], P('dp', 'seq'), may hold values from -22 to 22
- key_rows: bfloat16 [16, 4096, 2048], P('dp', 'seq'), may hold values from -7 to 7
- value_rows: bfloat16 [16, 4096, 2048], P('dp', 'seq'), may hold values from -6 to 6
- sink_logit: float32 [16], replicated, may hold values from 6 to 11
- grad_out: bfloat16 [16, 4096, 2048], P('dp', 'seq'), may hold values from -1.6 to 1.6
- pattern: int32 [16, 32, 8], replicated, may hold values from 0 to 31, as said below
Outputs:
- attended: bfloat16 [16, 4096, 2048], P('dp', 'seq')
- grad_query: bfloat16 [16, 4096, 2048], P('dp', 'seq')
- grad_key: bfloat16 [16, 4096, 2048], P('dp', 'seq')
- grad_value: bfloat16 [16, 4096, 2048], P('dp', 'seq')
- grad_sink: float32 [16], replicated
Inputs may be any that keep to these rules, and one draw needn't show every extreme that they name: For each head h and query block b, pattern[h, b] lists 8 distinct key blocks: the three neighbouring blocks b - 1, b, b + 1 (moved inward at the ends of the document), the first and the last block, and blocks drawn at random to fill the row.
All inputs are finite; a program needn't handle non-finite values.
Results may differ from a plain program's by a relative error of at most 0.012.
The roundings to bfloat16 on the way count: a program that leaves them out, or rounds other values in their place, can miss the bound.
Values may be sent and summed in bfloat16 or wider, within the bound.
No kernel may reach another device: no remote copies, remote signals or barrier semaphores. Data moves between devices by JAX's collectives and lax.ppermute only.
A program may use at most 64 MiB of HBM per device.

v0:
```python
import jax
import jax.numpy as jnp
from jax import lax
from jax.sharding import PartitionSpec as P

HEAD = 128
BLOCK = 128


tile_group = 4


def tile_scores(queries, key_tiles, scaling):
    return (
        jnp.einsum("gqe,gkbe->gqkb", queries, key_tiles, preferred_element_type=jnp.float32)
        * scaling
    )


def log_totals(scores, sink_value):
    row_top = jnp.maximum(jnp.max(scores, axis=(2, 3)), sink_value)
    summed = jnp.sum(jnp.exp(scores - row_top[:, :, None, None]), axis=(2, 3)) + jnp.exp(
        sink_value - row_top
    )
    return row_top + jnp.log(summed)


def softmax_weights(scores, log_total):
    weights = jnp.exp(scores - log_total[:, :, None, None])
    return (weights, weights.astype(jnp.bfloat16))


def attend(rounded, value_tiles):
    return jnp.einsum(
        "gqkb,gkbe->gqe", rounded, value_tiles, preferred_element_type=jnp.float32
    ).astype(jnp.bfloat16)


def gradients(
    weights,
    rounded,
    attended,
    queries,
    key_tiles,
    value_tiles,
    grad_tile,
    log_total,
    sink_value,
    scaling,
):
    row_dot = jnp.sum(grad_tile.astype(jnp.float32) * attended.astype(jnp.float32), axis=-1)
    grad_weights = jnp.einsum(
        "gqe,gkbe->gqkb", grad_tile, value_tiles, preferred_element_type=jnp.float32
    )
    grad_scores = (weights * (grad_weights - row_dot[:, :, None, None])).astype(jnp.bfloat16)
    grad_query = (
        jnp.einsum("gqkb,gkbe->gqe", grad_scores, key_tiles, preferred_element_type=jnp.float32)
        * scaling
    ).astype(jnp.bfloat16)
    key_part = (
        jnp.einsum("gqkb,gqe->gkbe", grad_scores, queries, preferred_element_type=jnp.float32)
        * scaling
    )
    value_part = jnp.einsum(
        "gqkb,gqe->gkbe", rounded, grad_tile, preferred_element_type=jnp.float32
    )
    sink_part = -jnp.sum(jnp.exp(sink_value - log_total) * row_dot)
    return (grad_query, key_part, value_part, sink_part)


def head_tiles(array_in, head_index):
    row_count = array_in.shape[0]
    picked = lax.dynamic_index_in_dim(array_in, head_index, 1, keepdims=False)
    return picked.reshape(row_count // BLOCK, BLOCK, HEAD)


def put_head(tiles):
    return tiles.reshape(-1, 1, HEAD)


def group_rows(tiles, group_index):
    return lax.dynamic_slice_in_dim(tiles, group_index * tile_group, tile_group, 0)


def put_group(buffer, tiles, group_index):
    return lax.dynamic_update_slice_in_dim(buffer, tiles, group_index * tile_group, 0)


def put_scalar(value_in):
    return value_in[None]


def forward_pass(query_heads, key_heads, value_heads, head_links, head_sinks, scaling):
    row_count, local_heads, _ = query_heads.shape
    block_count = row_count // BLOCK

    def forward_one_head(head_index, head_state):
        query_tiles = head_tiles(query_heads, head_index)
        key_all = head_tiles(key_heads, head_index)
        value_all = head_tiles(value_heads, head_index)
        link_rows = lax.dynamic_index_in_dim(head_links, head_index, 0, keepdims=False)
        sink_value = lax.dynamic_index_in_dim(head_sinks, head_index, 0, keepdims=False)

        def forward_one_group(group_index, inner_state):
            out_tiles, total_tiles = inner_state
            chosen = group_rows(link_rows, group_index)
            scores = tile_scores(group_rows(query_tiles, group_index), key_all[chosen], scaling)
            group_total = log_totals(scores, sink_value)
            _, rounded = softmax_weights(scores, group_total)
            result = attend(rounded, value_all[chosen])
            return (
                put_group(out_tiles, result, group_index),
                put_group(total_tiles, group_total, group_index),
            )

        initial = (
            jnp.zeros((block_count, BLOCK, HEAD), jnp.bfloat16),
            jnp.zeros((block_count, BLOCK), jnp.float32),
        )
        out_tiles, total_tiles = lax.fori_loop(
            0, block_count // tile_group, forward_one_group, initial
        )
        return (put_head(out_tiles), total_tiles[None])

    initial = (
        jnp.zeros((row_count, local_heads, HEAD), jnp.bfloat16),
        jnp.zeros((local_heads, block_count, BLOCK), jnp.float32),
    )
    return lax.fori_loop(0, local_heads, forward_one_head, initial)


def backward_pass(
    query_heads,
    key_heads,
    value_heads,
    grad_heads,
    attended,
    log_total,
    head_links,
    head_sinks,
    scaling,
):
    row_count, local_heads, _ = query_heads.shape
    block_count = row_count // BLOCK

    def backward_one_head(head_index, head_state):
        query_tiles = head_tiles(query_heads, head_index)
        key_all = head_tiles(key_heads, head_index)
        value_all = head_tiles(value_heads, head_index)
        grad_tiles = head_tiles(grad_heads, head_index)
        out_tiles = head_tiles(attended, head_index)
        head_total = lax.dynamic_index_in_dim(log_total, head_index, 0, keepdims=False)
        link_rows = lax.dynamic_index_in_dim(head_links, head_index, 0, keepdims=False)
        sink_value = lax.dynamic_index_in_dim(head_sinks, head_index, 0, keepdims=False)

        def backward_one_group(group_index, inner_state):
            query_part_all, key_acc, value_acc, sink_acc = inner_state
            chosen = group_rows(link_rows, group_index)
            queries = group_rows(query_tiles, group_index)
            key_tiles = key_all[chosen]
            value_tiles = value_all[chosen]
            group_total = group_rows(head_total, group_index)
            scores = tile_scores(queries, key_tiles, scaling)
            weights, rounded = softmax_weights(scores, group_total)
            grad_query, key_part, value_part, sink_part = gradients(
                weights,
                rounded,
                group_rows(out_tiles, group_index),
                queries,
                key_tiles,
                value_tiles,
                group_rows(grad_tiles, group_index),
                group_total,
                sink_value,
                scaling,
            )
            flat_links = chosen.reshape(-1)
            key_acc = key_acc.at[flat_links].add(key_part.reshape(-1, BLOCK, HEAD))
            value_acc = value_acc.at[flat_links].add(value_part.reshape(-1, BLOCK, HEAD))
            return (
                put_group(query_part_all, grad_query, group_index),
                key_acc,
                value_acc,
                sink_acc + sink_part,
            )

        initial = (
            jnp.zeros((block_count, BLOCK, HEAD), jnp.bfloat16),
            jnp.zeros((block_count, BLOCK, HEAD), jnp.float32),
            jnp.zeros((block_count, BLOCK, HEAD), jnp.float32),
            jnp.zeros((), jnp.float32),
        )
        query_part_all, key_acc, value_acc, sink_acc = lax.fori_loop(
            0, block_count // tile_group, backward_one_group, initial
        )
        return (
            put_head(query_part_all),
            put_head(key_acc.astype(jnp.bfloat16)),
            put_head(value_acc.astype(jnp.bfloat16)),
            put_scalar(sink_acc),
        )

    blank = jnp.zeros((row_count, local_heads, HEAD), jnp.bfloat16)
    initial = (blank, blank, blank, jnp.zeros((local_heads,), jnp.float32))
    return lax.fori_loop(0, local_heads, backward_one_head, initial)


def on_device(query_rows, key_rows, value_rows, sink_logit, grad_out, pattern):
    token_count = query_rows.shape[1]
    head_count = sink_logit.shape[0]
    local_heads = head_count // lax.axis_size("seq")
    first_head = lax.axis_index("seq") * local_heads
    head_links = lax.dynamic_slice_in_dim(pattern, first_head, local_heads, 0)
    head_sinks = lax.dynamic_slice_in_dim(sink_logit, first_head, local_heads, 0)
    scaling = HEAD ** (-0.5)

    def split_heads(array_in):
        return array_in.reshape(token_count, head_count, HEAD)

    def join_heads(array_in):
        return array_in.reshape(1, token_count, head_count * HEAD)

    query_heads, key_heads, value_heads = (
        lax.all_to_all(split_heads(query_rows), "seq", split_axis=1, concat_axis=0, tiled=True),
        lax.all_to_all(split_heads(key_rows), "seq", split_axis=1, concat_axis=0, tiled=True),
        lax.all_to_all(split_heads(value_rows), "seq", split_axis=1, concat_axis=0, tiled=True),
    )
    attended_heads, log_total = forward_pass(
        query_heads, key_heads, value_heads, head_links, head_sinks, scaling
    )
    attended = lax.all_to_all(attended_heads, "seq", split_axis=0, concat_axis=1, tiled=True)
    grad_heads = lax.all_to_all(
        split_heads(grad_out), "seq", split_axis=1, concat_axis=0, tiled=True
    )
    query_grads, key_grads, value_grads, sink_terms = backward_pass(
        query_heads,
        key_heads,
        value_heads,
        grad_heads,
        attended_heads,
        log_total,
        head_links,
        head_sinks,
        scaling,
    )
    grad_query, grad_key, grad_value = (
        lax.all_to_all(query_grads, "seq", split_axis=0, concat_axis=1, tiled=True),
        lax.all_to_all(key_grads, "seq", split_axis=0, concat_axis=1, tiled=True),
        lax.all_to_all(value_grads, "seq", split_axis=0, concat_axis=1, tiled=True),
    )
    spread = lax.dynamic_update_slice_in_dim(
        jnp.zeros((head_count,), jnp.float32), sink_terms, first_head, 0
    )
    summed = lax.psum(spread, ("seq", "dp"))
    grad_sink = summed / lax.axis_size("dp")
    return (
        join_heads(attended),
        join_heads(grad_query),
        join_heads(grad_key),
        join_heads(grad_value),
        grad_sink,
    )


def solution(mesh):
    placed = (
        P("dp", "seq", None),
        P("dp", "seq", None),
        P("dp", "seq", None),
        P(),
        P("dp", "seq", None),
        P(),
    )
    return jax.shard_map(
        on_device,
        mesh=mesh,
        in_specs=placed,
        out_specs=(
            P("dp", "seq", None),
            P("dp", "seq", None),
            P("dp", "seq", None),
            P("dp", "seq", None),
            P(),
        ),
        check_vma=False,
    )
```

profile of v0, /device:TPU:64, one launch (start us, length us, event | category | flops | bytes accessed | tf_op | source)
XLA Modules:
  0.0 534.3 jit_solution(4679714297359195096)
XLA Ops:
  3.4 7.1 %all-to-all-start = ((bf16[256,16,128]{2,0,1:T(8,128)(2,1)}), bf16[256,16,128]{2,0,1:T(8,128)(2,1)}, u32[]{:S(2)}, u32[]{:S(2)}) async-start(bf16[256,16,128]{2,0,1:T(8,128)(2,1)} %copy.62), calls=%async_computation | async-start | bytes 2097152 | tf_op jit(solution)/shard_map/all_to_all | solution.py:224
  12.0 16.3 %all-to-all-done = bf16[256,16,128]{2,0,1:T(8,128)(2,1)} async-done(((bf16[256,16,128]{2,0,1:T(8,128)(2,1)}), bf16[256,16,128]{2,0,1:T(8,128)(2,1)}, u32[]{:S(2)}, u32[]{:S(2)}) %all-to-all-start) | async-done | bytes 1048608 | tf_op jit(solution)/shard_map/all_to_all | solution.py:224
  33.4 13.7 %all-to-all-done.1 = bf16[256,16,128]{2,0,1:T(8,128)(2,1)S(1)} async-done(((bf16[256,16,128]{2,0,1:T(8,128)(2,1)}), bf16[256,16,128]{2,0,1:T(8,128)(2,1)S(1)}, u32[]{:S(2)}, u32[]{:S(2)}) %all-to-all-start.1) | async-done | bytes 1048608 | tf_op jit(solution)/shard_map/all_to_all | solution.py:225
  52.9 13.8 %all-to-all-done.2 = bf16[256,16,128]{2,0,1:T(8,128)(2,1)S(1)} async-done(((bf16[256,16,128]{2,0,1:T(8,128)(2,1)}), bf16[256,16,128]{2,0,1:T(8,128)(2,1)S(1)}, u32[]{:S(2)}, u32[]{:S(2)}) %all-to-all-start.2) | async-done | bytes 1048608 | tf_op jit(solution)/shard_map/all_to_all | solution.py:226
  66.7 4.4 all-to-all-start.4
  72.3 56.4 %while.58 = (s32[]{:T(128)}, bf16[32,128,128]{2,1,0:T(8,128)(2,1)}, f32[32,128]{1,0:T(8,128)S(1)}, bf16[32,128,128]{2,1,0:T(8,128)(2,1)}, s32[32,8]{1,0:T(8,128)...) while((s32[]{:T(128)}, bf16[32,128,128]{2,1,0:T(8,128)(2,1)}, ...), condition=%wide.region_3.4_spmd, body=%wide.region_0.3_spmd.sunk | while | flops 272697952 | bytes 12870715 | solution.py:120
  133.0 7.2 %all-to-all-start.3 = ((bf16[16,2,16384]{2,1,0:T(2,128)(2,1)}), bf16[16,2,16384]{2,1,0:T(2,128)(2,1)}, u32[]{:S(2)}, u32[]{:S(2)}) async-start(bf16[16,2,16384]{2,1,0:T(2,128)(2,1)} %reshape.236), calls=%async_computation.3 | async-start | bytes 2097152 | tf_op jit(solution)/shard_map/all_to_all | solution.py:231
  144.5 237.5 %while.59 = (s32[]{:T(128)}, bf16[32,128,128]{2,1,0:T(8,128)(2,1)}, f32[32,128,128]{2,1,0:T(8,128)}, f32[32,128,128]{2,1,0:T(8,128)}, f32[]{:T(128)}, /*index=5*...) while((s32[]{:T(128)}, bf16[32,128,128]{2,1,0:T(8,128)(2,1)}, ...), condition=%wide.region_9.10_spmd, body=%wide.region_4.9_spmd.sunk | while | flops 677251264 | bytes 47075420 | solution.py:193
  156.3 7.0 %scatter_fusion.1 = f32[32,128,128]{2,1,0:T(8,128)} fusion(f32[32,128,128]{2,1,0:T(8,128)} %get-tuple-element.721, s32[32]{0:T(128)S(1)} %fusion.71, f32[32,128,128]{2,1,0:T(8,128)} %bitcast.152), kind=kCustom, calls=%fused_computation.5.clone.1 | custom fusion | flops 524288 | bytes 6291584 | tf_op jit(solution)/shard_map/while/body/eval_jaxpr/while/body/eval_jaxpr/scatter-add | solution.py:179
  167.2 7.0 %scatter_fusion = f32[32,128,128]{2,1,0:T(8,128)} fusion(f32[32,128,128]{2,1,0:T(8,128)} %get-tuple-element.720, s32[32]{0:T(128)S(1)} %fusion.71, f32[32,128,128]{2,1,0:T(8,128)} %bitcast.151), kind=kCustom, calls=%fused_computation.4.clone.1 | custom fusion | flops 524288 | bytes 6291584 | tf_op jit(solution)/shard_map/while/body/eval_jaxpr/while/body/eval_jaxpr/scatter-add | solution.py:178
  186.0 7.0 %scatter_fusion.1 = f32[32,128,128]{2,1,0:T(8,128)} fusion(f32[32,128,128]{2,1,0:T(8,128)} %get-tuple-element.721, s32[32]{0:T(128)S(1)} %fusion.71, f32[32,128,128]{2,1,0:T(8,128)} %bitcast.152), kind=kCustom, calls=%fused_computation.5.clone.1 | custom fusion | flops 524288 | bytes 6291584 | tf_op jit(solution)/shard_map/while/body/eval_jaxpr/while/body/eval_jaxpr/scatter-add | solution.py:179
  196.8 7.0 %scatter_fusion = f32[32,128,128]{2,1,0:T(8,128)} fusion(f32[32,128,128]{2,1,0:T(8,128)} %get-tuple-element.720, s32[32]{0:T(128)S(1)} %fusion.71, f32[32,128,128]{2,1,0:T(8,128)} %bitcast.151), kind=kCustom, calls=%fused_computation.4.clone.1 | custom fusion | flops 524288 | bytes 6291584 | tf_op jit(solution)/shard_map/while/body/eval_jaxpr/while/body/eval_jaxpr/scatter-add | solution.py:178
  215.7 7.0 %scatter_fusion.1 = f32[32,128,128]{2,1,0:T(8,128)} fusion(f32[32,128,128]{2,1,0:T(8,128)} %get-tuple-element.721, s32[32]{0:T(128)S(1)} %fusion.71, f32[32,128,128]{2,1,0:T(8,128)} %bitcast.152), kind=kCustom, calls=%fused_computation.5.clone.1 | custom fusion | flops 524288 | bytes 6291584 | tf_op jit(solution)/shard_map/while/body/eval_jaxpr/while/body/eval_jaxpr/scatter-add | solution.py:179
  226.5 7.0 %scatter_fusion = f32[32,128,128]{2,1,0:T(8,128)} fusion(f32[32,128,128]{2,1,0:T(8,128)} %get-tuple-element.720, s32[32]{0:T(128)S(1)} %fusion.71, f32[32,128,128]{2,1,0:T(8,128)} %bitcast.151), kind=kCustom, calls=%fused_computation.4.clone.1 | custom fusion | flops 524288 | bytes 6291584 | tf_op jit(solution)/shard_map/while/body/eval_jaxpr/while/body/eval_jaxpr/scatter-add | solution.py:178
  245.4 7.0 %scatter_fusion.1 = f32[32,128,128]{2,1,0:T(8,128)} fusion(f32[32,128,128]{2,1,0:T(8,128)} %get-tuple-element.721, s32[32]{0:T(128)S(1)} %fusion.71, f32[32,128,128]{2,1,0:T(8,128)} %bitcast.152), kind=kCustom, calls=%fused_computation.5.clone.1 | custom fusion | flops 524288 | bytes 6291584 | tf_op jit(solution)/shard_map/while/body/eval_jaxpr/while/body/eval_jaxpr/scatter-add | solution.py:179
  256.2 7.0 %scatter_fusion = f32[32,128,128]{2,1,0:T(8,128)} fusion(f32[32,128,128]{2,1,0:T(8,128)} %get-tuple-element.720, s32[32]{0:T(128)S(1)} %fusion.71, f32[32,128,128]{2,1,0:T(8,128)} %bitcast.151), kind=kCustom, calls=%fused_computation.4.clone.1 | custom fusion | flops 524288 | bytes 6291584 | tf_op jit(solution)/shard_map/while/body/eval_jaxpr/while/body/eval_jaxpr/scatter-add | solution.py:178
  275.0 7.0 %scatter_fusion.1 = f32[32,128,128]{2,1,0:T(8,128)} fusion(f32[32,128,128]{2,1,0:T(8,128)} %get-tuple-element.721, s32[32]{0:T(128)S(1)} %fusion.71, f32[32,128,128]{2,1,0:T(8,128)} %bitcast.152), kind=kCustom, calls=%fused_computation.5.clone.1 | custom fusion | flops 524288 | bytes 6291584 | tf_op jit(solution)/shard_map/while/body/eval_jaxpr/while/body/eval_jaxpr/scatter-add | solution.py:179
  285.9 7.0 %scatter_fusion = f32[32,128,128]{2,1,0:T(8,128)} fusion(f32[32,128,128]{2,1,0:T(8,128)} %get-tuple-element.720, s32[32]{0:T(128)S(1)} %fusion.71, f32[32,128,128]{2,1,0:T(8,128)} %bitcast.151), kind=kCustom, calls=%fused_computation.4.clone.1 | custom fusion | flops 524288 | bytes 6291584 | tf_op jit(solution)/shard_map/while/body/eval_jaxpr/while/body/eval_jaxpr/scatter-add | solution.py:178
  304.7 7.0 %scatter_fusion.1 = f32[32,128,128]{2,1,0:T(8,128)} fusion(f32[32,128,128]{2,1,0:T(8,128)} %get-tuple-element.721, s32[32]{0:T(128)S(1)} %fusion.71, f32[32,128,128]{2,1,0:T(8,128)} %bitcast.152), kind=kCustom, calls=%fused_computation.5.clone.1 | custom fusion | flops 524288 | bytes 6291584 | tf_op jit(solution)/shard_map/while/body/eval_jaxpr/while/body/eval_jaxpr/scatter-add | solution.py:179
  315.6 7.0 %scatter_fusion = f32[32,128,128]{2,1,0:T(8,128)} fusion(f32[32,128,128]{2,1,0:T(8,128)} %get-tuple-element.720, s32[32]{0:T(128)S(1)} %fusion.71, f32[32,128,128]{2,1,0:T(8,128)} %bitcast.151), kind=kCustom, calls=%fused_computation.4.clone.1 | custom fusion | flops 524288 | bytes 6291584 | tf_op jit(solution)/shard_map/while/body/eval_jaxpr/while/body/eval_jaxpr/scatter-add | solution.py:178
  334.4 7.0 %scatter_fusion.1 = f32[32,128,128]{2,1,0:T(8,128)} fusion(f32[32,128,128]{2,1,0:T(8,128)} %get-tuple-element.721, s32[32]{0:T(128)S(1)} %fusion.71, f32[32,128,128]{2,1,0:T(8,128)} %bitcast.152), kind=kCustom, calls=%fused_computation.5.clone.1 | custom fusion | flops 524288 | bytes 6291584 | tf_op jit(solution)/shard_map/while/body/eval_jaxpr/while/body/eval_jaxpr/scatter-add | solution.py:179
  345.3 7.0 %scatter_fusion = f32[32,128,128]{2,1,0:T(8,128)} fusion(f32[32,128,128]{2,1,0:T(8,128)} %get-tuple-element.720, s32[32]{0:T(128)S(1)} %fusion.71, f32[32,128,128]{2,1,0:T(8,128)} %bitcast.151), kind=kCustom, calls=%fused_computation.4.clone.1 | custom fusion | flops 524288 | bytes 6291584 | tf_op jit(solution)/shard_map/while/body/eval_jaxpr/while/body/eval_jaxpr/scatter-add | solution.py:178
  364.1 7.0 %scatter_fusion.1 = f32[32,128,128]{2,1,0:T(8,128)} fusion(f32[32,128,128]{2,1,0:T(8,128)} %get-tuple-element.721, s32[32]{0:T(128)S(1)} %fusion.71, f32[32,128,128]{2,1,0:T(8,128)} %bitcast.152), kind=kCustom, calls=%fused_computation.5.clone.1 | custom fusion | flops 524288 | bytes 6291584 | tf_op jit(solution)/shard_map/while/body/eval_jaxpr/while/body/eval_jaxpr/scatter-add | solution.py:179
  375.0 7.0 %scatter_fusion = f32[32,128,128]{2,1,0:T(8,128)} fusion(f32[32,128,128]{2,1,0:T(8,128)} %get-tuple-element.720, s32[32]{0:T(128)S(1)} %fusion.71, f32[32,128,128]{2,1,0:T(8,128)} %bitcast.151), kind=kCustom, calls=%fused_computation.4.clone.1 | custom fusion | flops 524288 | bytes 6291584 | tf_op jit(solution)/shard_map/while/body/eval_jaxpr/while/body/eval_jaxpr/scatter-add | solution.py:178
  385.8 7.3 %all-to-all-start.5 = ((bf16[16,2,16384]{2,1,0:T(2,128)(2,1)}), bf16[16,2,16384]{2,1,0:T(2,128)(2,1)}, u32[]{:S(2)}, u32[]{:S(2)}) async-start(bf16[16,2,16384]{2,1,0:T(2,128)(2,1)} %reshape.238), calls=%async_computation.5 | async-start | bytes 2097152 | tf_op jit(solution)/shard_map/all_to_all | solution.py:247
  397.7 9.6 %all-to-all-done.5 = bf16[16,2,16384]{2,1,0:T(2,128)(2,1)} async-done(((bf16[16,2,16384]{2,1,0:T(2,128)(2,1)}), bf16[16,2,16384]{2,1,0:T(2,128)(2,1)}, u32[]{:S(2)}, u32[]{:S(2)}) %all-to-all-start.5) | async-done | bytes 1048608 | tf_op jit(solution)/shard_map/all_to_all | solution.py:247
  407.2 4.3 all-to-all-start.6
  414.4 10.2 %all-to-all-done.6 = bf16[16,2,16384]{2,1,0:T(2,128)(2,1)} async-done(((bf16[16,2,16384]{2,1,0:T(2,128)(2,1)}), bf16[16,2,16384]{2,1,0:T(2,128)(2,1)}, u32[]{:S(2)}, u32[]{:S(2)}) %all-to-all-start.6) | async-done | bytes 1048608 | tf_op jit(solution)/shard_map/all_to_all | solution.py:248
  428.3 77.3 %psum.7 = f32[16]{0:T(128)S(1)} all-reduce(f32[16]{0:T(128)S(1)} %dynamic_update_slice.24), channel_id=1, replica_groups=mesh['seq'=16,'dp'=16] {'seq','dp'}, use_global_device_ids=true, to_apply=%region_10.11 | all-reduce | flops 16 | bytes 128 | tf_op jit(solution)/shard_map/psum | solution.py:254
  506.1 4.3 reshape.237
  514.5 4.3 reshape.239
  522.8 4.3 reshape.241
  (305 shorter events, 231.5 us)
Async XLA Ops:
  0.6 50.7 %copy-start = (s32[16,32,8]{1,2,0:T(8,128)S(1)}, s32[16,32,8]{1,2,0:T(8,128)}, u32[]{:S(2)}) copy-start(s32[16,32,8]{1,2,0:T(8,128)} %param.15) | copy-start | bytes 49156
  2.1 8.4 %copy-start.7 = (bf16[1,256,2048]{2,1,0:T(8,128)(2,1)S(1)}, bf16[1,256,2048]{2,1,0:T(8,128)(2,1)}, u32[]{:S(2)}) copy-start(bf16[1,256,2048]{2,1,0:T(8,128)(2,1)} %param.11) | copy-start | bytes 3145732
  3.4 24.8 %all-to-all-start = ((bf16[256,16,128]{2,0,1:T(8,128)(2,1)}), bf16[256,16,128]{2,0,1:T(8,128)(2,1)}, u32[]{:S(2)}, u32[]{:S(2)}) async-start(bf16[256,16,128]{2,0,1:T(8,128)(2,1)} %copy.62), calls=%async_computation | async-start | bytes 2097152 | tf_op jit(solution)/shard_map/all_to_all | solution.py:224
  10.7 21.2 %copy-start.8 = (bf16[1,256,2048]{2,1,0:T(8,128)(2,1)S(1)}, bf16[1,256,2048]{2,1,0:T(8,128)(2,1)}, u32[]{:S(2)}) copy-start(bf16[1,256,2048]{2,1,0:T(8,128)(2,1)} %param.12) | copy-start | bytes 3145732
  28.2 18.9 %all-to-all-start.1 = ((bf16[256,16,128]{2,0,1:T(8,128)(2,1)}), bf16[256,16,128]{2,0,1:T(8,128)(2,1)S(1)}, u32[]{:S(2)}, u32[]{:S(2)}) async-start(bf16[256,16,128]{2,0,1:T(8,128)(2,1)} %copy.64), calls=%async_computation.1 | async-start | bytes 2097152 | tf_op jit(solution)/shard_map/all_to_all | solution.py:225
  32.1 18.7 %copy-start.10 = (f32[16]{0:T(128)S(1)}, f32[16]{0:T(128)}, u32[]{:S(2)}) copy-start(f32[16]{0:T(128)} %param.13) | copy-start | bytes 196
  32.2 19.3 %copy-start.9 = (bf16[1,256,2048]{2,1,0:T(8,128)(2,1)S(1)}, bf16[1,256,2048]{2,1,0:T(8,128)(2,1)}, u32[]{:S(2)}) copy-start(bf16[1,256,2048]{2,1,0:T(8,128)(2,1)} %param.14) | copy-start | bytes 3145732
  47.1 19.6 %all-to-all-start.2 = ((bf16[256,16,128]{2,0,1:T(8,128)(2,1)}), bf16[256,16,128]{2,0,1:T(8,128)(2,1)S(1)}, u32[]{:S(2)}, u32[]{:S(2)}) async-start(bf16[256,16,128]{2,0,1:T(8,128)(2,1)} %copy.65), calls=%async_computation.2 | async-start | bytes 2097152 | tf_op jit(solution)/shard_map/all_to_all | solution.py:226
  66.7 66.3 %all-to-all-start.4 = ((bf16[256,16,128]{2,0,1:T(8,128)(2,1)}), bf16[256,16,128]{2,0,1:T(8,128)(2,1)}, u32[]{:S(2)}, u32[]{:S(2)}) async-start(bf16[256,16,128]{2,0,1:T(8,128)(2,1)} %copy.68), calls=%async_computation.4 | async-start | bytes 2097152 | tf_op jit(solution)/shard_map/all_to_all | solution.py:232
  133.0 252.8 %all-to-all-start.3 = ((bf16[16,2,16384]{2,1,0:T(2,128)(2,1)}), bf16[16,2,16384]{2,1,0:T(2,128)(2,1)}, u32[]{:S(2)}, u32[]{:S(2)}) async-start(bf16[16,2,16384]{2,1,0:T(2,128)(2,1)} %reshape.236), calls=%async_computation.3 | async-start | bytes 2097152 | tf_op jit(solution)/shard_map/all_to_all | solution.py:231
  144.5 5.1 copy-start.2
  167.2 7.0 %copy-start.3 = (bf16[32,128,128]{2,1,0:T(8,128)(2,1)S(1)}, bf16[32,128,128]{2,1,0:T(8,128)(2,1)}, u32[]{:S(2)}) copy-start(bf16[32,128,128]{2,1,0:T(8,128)(2,1)} %copy-done.2) | copy-start | bytes 3145732 | tf_op jit(solution)/shard_map/while/body/eval_jaxpr/while
  174.2 5.1 copy-start.2
  196.8 7.0 %copy-start.3 = (bf16[32,128,128]{2,1,0:T(8,128)(2,1)S(1)}, bf16[32,128,128]{2,1,0:T(8,128)(2,1)}, u32[]{:S(2)}) copy-start(bf16[32,128,128]{2,1,0:T(8,128)(2,1)} %copy-done.2) | copy-start | bytes 3145732 | tf_op jit(solution)/shard_map/while/body/eval_jaxpr/while
  203.9 5.1 copy-start.2
  226.5 7.0 %copy-start.3 = (bf16[32,128,128]{2,1,0:T(8,128)(2,1)S(1)}, bf16[32,128,128]{2,1,0:T(8,128)(2,1)}, u32[]{:S(2)}) copy-start(bf16[32,128,128]{2,1,0:T(8,128)(2,1)} %copy-done.2) | copy-start | bytes 3145732 | tf_op jit(solution)/shard_map/while/body/eval_jaxpr/while
  233.5 5.1 copy-start.2
  256.2 7.0 %copy-start.3 = (bf16[32,128,128]{2,1,0:T(8,128)(2,1)S(1)}, bf16[32,128,128]{2,1,0:T(8,128)(2,1)}, u32[]{:S(2)}) copy-start(bf16[32,128,128]{2,1,0:T(8,128)(2,1)} %copy-done.2) | copy-start | bytes 3145732 | tf_op jit(solution)/shard_map/while/body/eval_jaxpr/while
  263.2 5.1 copy-start.2
  285.9 7.0 %copy-start.3 = (bf16[32,128,128]{2,1,0:T(8,128)(2,1)S(1)}, bf16[32,128,128]{2,1,0:T(8,128)(2,1)}, u32[]{:S(2)}) copy-start(bf16[32,128,128]{2,1,0:T(8,128)(2,1)} %copy-done.2) | copy-start | bytes 3145732 | tf_op jit(solution)/shard_map/while/body/eval_jaxpr/while
  292.9 5.1 copy-start.2
  315.6 7.0 %copy-start.3 = (bf16[32,128,128]{2,1,0:T(8,128)(2,1)S(1)}, bf16[32,128,128]{2,1,0:T(8,128)(2,1)}, u32[]{:S(2)}) copy-start(bf16[32,128,128]{2,1,0:T(8,128)(2,1)} %copy-done.2) | copy-start | bytes 3145732 | tf_op jit(solution)/shard_map/while/body/eval_jaxpr/while
  322.6 5.1 copy-start.2
  345.3 7.0 %copy-start.3 = (bf16[32,128,128]{2,1,0:T(8,128)(2,1)S(1)}, bf16[32,128,128]{2,1,0:T(8,128)(2,1)}, u32[]{:S(2)}) copy-start(bf16[32,128,128]{2,1,0:T(8,128)(2,1)} %copy-done.2) | copy-start | bytes 3145732 | tf_op jit(solution)/shard_map/while/body/eval_jaxpr/while
  352.3 5.1 copy-start.2
  375.0 7.0 %copy-start.3 = (bf16[32,128,128]{2,1,0:T(8,128)(2,1)S(1)}, bf16[32,128,128]{2,1,0:T(8,128)(2,1)}, u32[]{:S(2)}) copy-start(bf16[32,128,128]{2,1,0:T(8,128)(2,1)} %copy-done.2) | copy-start | bytes 3145732 | tf_op jit(solution)/shard_map/while/body/eval_jaxpr/while
  384.7 8.4 %copy-start.6 = (f32[32,128,128]{2,1,0:T(8,128)S(1)}, f32[32,128,128]{2,1,0:T(8,128)}, u32[]{:S(2)}) copy-start(f32[32,128,128]{2,1,0:T(8,128)} %get-tuple-element.453) | copy-start | bytes 6291460
  385.8 21.4 %all-to-all-start.5 = ((bf16[16,2,16384]{2,1,0:T(2,128)(2,1)}), bf16[16,2,16384]{2,1,0:T(2,128)(2,1)}, u32[]{:S(2)}, u32[]{:S(2)}) async-start(bf16[16,2,16384]{2,1,0:T(2,128)(2,1)} %reshape.238), calls=%async_computation.5 | async-start | bytes 2097152 | tf_op jit(solution)/shard_map/all_to_all | solution.py:247
  395.4 16.2 %copy-start.5 = (f32[32,128,128]{2,1,0:T(8,128)S(1)}, f32[32,128,128]{2,1,0:T(8,128)}, u32[]{:S(2)}) copy-start(f32[32,128,128]{2,1,0:T(8,128)} %get-tuple-element.454) | copy-start | bytes 6291460
  407.2 17.3 %all-to-all-start.6 = ((bf16[16,2,16384]{2,1,0:T(2,128)(2,1)}), bf16[16,2,16384]{2,1,0:T(2,128)(2,1)}, u32[]{:S(2)}, u32[]{:S(2)}) async-start(bf16[16,2,16384]{2,1,0:T(2,128)(2,1)} %reshape.240), calls=%async_computation.6 | async-start | bytes 2097152 | tf_op jit(solution)/shard_map/all_to_all | solution.py:248
  424.5 106.6 %all-to-all-start.7 = ((bf16[16,2,16384]{2,1,0:T(2,128)(2,1)}), bf16[16,2,16384]{2,1,0:T(2,128)(2,1)S(1)}, u32[]{:S(2)}, u32[]{:S(2)}) async-start(bf16[16,2,16384]{2,1,0:T(2,128)(2,1)} %reshape.242), calls=%async_computation.7 | async-start | bytes 2097152 | tf_op jit(solution)/shard_map/all_to_all | solution.py:249
  532.3 2.0 copy-start.1
  (8 other events, 11.6 us)
where the time goes:
time: 542 us; the launch traced here: 534 us
  other arithmetic  154 us (28%)
  matrix products  103 us (19%)
  local copies, waits for them, and re-layouts  88.2 us (16%)
  blocking collectives  77.3 us (14%)
  waiting for transfers between devices  63.5 us (12%)
  starting transfers between devices  41.2 us (8%)
  loops' own time  5.86 us (1%)
    psum x1, blocking collectives, on_device(): summed = lax.psum(spread, ('seq', 'dp'))  77.3 us
    scatter-add x8, other arithmetic, backward_one_group(): key_acc = key_acc.at[flat_links].add(key_part.reshape(-1, BLOCK, HEAD))  56.1 us
    scatter-add x8, other arithmetic, backward_one_group(): value_acc.at[flat_links].add(value_part.reshape(-1, BLOCK, HEAD))  56 us
    unnamed x36, local copies, waits for them, and re-layouts  30.9 us
    dot_general x16, matrix products, tile_scores(): jnp.einsum('gqe,gkbe->gqkb', queries, key_tiles, preferred_element_type=j...  25.5 us
    dot_general x8, matrix products, gradients(): jnp.einsum('gqkb,gqe->gkbe', rounded, grad_tile, preferred_element_type=j...  23.6 us
    dot_general x8, matrix products, gradients(): jnp.einsum('gqkb,gqe->gkbe', grad_scores, queries, preferred_element_type...  22.1 us
    all_to_all x1, waiting for transfers between devices, on_device(): lax.all_to_all(split_heads(query_rows), 'seq', split_axis=1, concat_axis=...  16.3 us
  transfers between devices with their start and end apart: 8, of which 5 were waited for; matrix products, arithmetic and copies ran while one was open for 64% of the time, Pallas kernels for 0%

commit v1 on v0

v1 whole, which is shorter than its diff:
```python
import functools

import jax
import jax.numpy as jnp
from jax import lax
from jax.experimental import pallas as pl
from jax.experimental.pallas import tpu as pltpu
from jax.sharding import PartitionSpec as P

HEAD = 128
BLOCK = 128
LOG2E = 1.4426950408889634
F32 = jnp.float32
BF16 = jnp.bfloat16

NT = (((1,), (1,)), ((), ()))
NN = (((1,), (0,)), ((), ()))
VMEM_WHOLE = pl.BlockSpec(memory_space=pltpu.VMEM)
SMEM_WHOLE = pl.BlockSpec(memory_space=pltpu.SMEM)
IN_PLACE = pl.BlockSpec(memory_space=pl.ANY)


def dot(left, right, dims):
    return lax.dot_general(left, right, dims, preferred_element_type=F32)


def tile(ref, block, part, per_device):
    rows = per_device * BLOCK
    half = lax.rem(block, per_device)
    start = pl.multiple_of(part * rows + half * BLOCK, BLOCK)
    return ref.at[lax.div(block, per_device), pl.ds(start, BLOCK), :]


def forward_kernel(blocks, slots, per_device, scaling, links, sink, rows, out, weights, sink_weight,
                   value_t, score):
    sink_value = sink[0]

    def flip(c, carry):
        value_t[c] = tile(rows, c, 2, per_device)[...].T
        return carry

    lax.fori_loop(0, blocks, flip, 0)

    def one_block(b, carry):
        queries = tile(rows, b, 0, per_device)[...]
        chosen = [links[b * slots + j] for j in range(slots)]
        top = None
        for j, c in enumerate(chosen):
            part = dot(tile(rows, c, 1, per_device)[...], queries, NT)
            score[pl.ds(j * BLOCK, BLOCK), :] = part
            part_top = jnp.max(part, axis=0, keepdims=True)
            top = part_top if top is None else jnp.maximum(top, part_top)
        top = jnp.maximum(top * scaling, sink_value)
        shift = top * LOG2E
        total = jnp.exp(sink_value - top)
        sink_part = total
        for j in range(slots):
            part = jnp.exp2(score[pl.ds(j * BLOCK, BLOCK), :] * (scaling * LOG2E) - shift)
            score[pl.ds(j * BLOCK, BLOCK), :] = part
            total = total + jnp.sum(part, axis=0, keepdims=True)
        inverse = 1.0 / total
        for j in range(slots):
            weights[b, pl.ds(j * BLOCK, BLOCK), :] = (
                score[pl.ds(j * BLOCK, BLOCK), :] * inverse).astype(BF16)
        values = jnp.concatenate([value_t[c] for c in chosen], axis=1)
        result = dot(values, weights[b], NN)
        tile(out, b, 0, per_device)[...] = result.T.astype(BF16)
        sink_weight[pl.ds(b, 1), :] = sink_part * inverse
        return carry

    lax.fori_loop(0, blocks, one_block, 0)


def backward_kernel(blocks, slots, per_device, scaling, links, rows, grads, attended, weights,
                    sink_weight, out, sink_out, key_t, change, key_sum, value_sum):
    def prepare(c, carry):
        key_t[c] = tile(rows, c, 1, per_device)[...].T
        key_sum[c] = jnp.zeros((BLOCK, HEAD), F32)
        value_sum[c] = jnp.zeros((BLOCK, HEAD), F32)
        return carry

    lax.fori_loop(0, blocks, prepare, 0)

    def one_block(b, sink_total):
        queries = tile(rows, b, 0, per_device)[...]
        grad = tile(grads, b, 0, per_device)[...]
        result = tile(attended, b, 0, per_device)[...]
        product = grad.astype(F32) * result.astype(F32)
        row_dot = jnp.sum(product.T, axis=0, keepdims=True)
        chosen = [links[b * slots + j] for j in range(slots)]
        for j, c in enumerate(chosen):
            weight = weights[b, pl.ds(j * BLOCK, BLOCK), :]
            grad_weight = dot(tile(rows, c, 2, per_device)[...], grad, NT)
            delta = (weight.astype(F32) * (grad_weight - row_dot)).astype(BF16)
            change[pl.ds(j * BLOCK, BLOCK), :] = delta
            value_sum[c] += dot(weight, grad, NN)
            key_sum[c] += dot(delta, queries, NN)
        keys = jnp.concatenate([key_t[c] for c in chosen], axis=1)
        grad_query = dot(keys, change[...], NN) * scaling
        tile(out, b, 0, per_device)[...] = grad_query.T.astype(BF16)
        return sink_total + row_dot * sink_weight[pl.ds(b, 1), :]

    sink_total = lax.fori_loop(0, blocks, one_block, jnp.zeros((1, BLOCK), F32))
    sink_out[...] = jnp.broadcast_to(sink_total, sink_out.shape)

    def finish(c, carry):
        tile(out, c, 1, per_device)[...] = (key_sum[c] * scaling).astype(BF16)
        tile(out, c, 2, per_device)[...] = value_sum[c].astype(BF16)
        return carry

    lax.fori_loop(0, blocks, finish, 0)


def forward(links, sink, rows, scaling, slots):
    peers, depth, _ = rows.shape
    tokens = depth // 3
    per_device = tokens // BLOCK
    blocks = peers * per_device
    return pl.pallas_call(
        functools.partial(forward_kernel, blocks, slots, per_device, scaling),
        out_shape=(
            jax.ShapeDtypeStruct((peers, tokens, HEAD), BF16),
            jax.ShapeDtypeStruct((blocks, slots * BLOCK, BLOCK), BF16),
            jax.ShapeDtypeStruct((blocks, BLOCK), F32),
        ),
        in_specs=[SMEM_WHOLE, SMEM_WHOLE, VMEM_WHOLE],
        out_specs=(VMEM_WHOLE, VMEM_WHOLE, VMEM_WHOLE),
        scratch_shapes=[
            pltpu.VMEM((blocks, HEAD, BLOCK), BF16),
            pltpu.VMEM((slots * BLOCK, BLOCK), F32),
        ],
        compiler_params=pltpu.CompilerParams(vmem_limit_bytes=40 << 20),
        cost_estimate=pl.CostEstimate(
            flops=4 * blocks * slots * BLOCK * BLOCK * HEAD,
            bytes_accessed=14 << 20,
            transcendentals=blocks * slots * BLOCK * BLOCK,
        ),
        name="forward",
    )(links, sink, rows)


def backward(links, rows, grads, attended, weights, sink_weight, scaling, slots):
    peers, tokens, _ = grads.shape
    per_device = tokens // BLOCK
    blocks = peers * per_device
    return pl.pallas_call(
        functools.partial(backward_kernel, blocks, slots, per_device, scaling),
        out_shape=(
            jax.ShapeDtypeStruct((peers, 3 * tokens, HEAD), BF16),
            jax.ShapeDtypeStruct((8, BLOCK), F32),
        ),
        in_specs=[SMEM_WHOLE] + [VMEM_WHOLE] * 5,
        out_specs=(VMEM_WHOLE, VMEM_WHOLE),
        scratch_shapes=[
            pltpu.VMEM((blocks, HEAD, BLOCK), BF16),
            pltpu.VMEM((slots * BLOCK, BLOCK), BF16),
            pltpu.VMEM((blocks, BLOCK, HEAD), F32),
            pltpu.VMEM((blocks, BLOCK, HEAD), F32),
        ],
        compiler_params=pltpu.CompilerParams(vmem_limit_bytes=40 << 20),
        cost_estimate=pl.CostEstimate(
            flops=8 * blocks * slots * BLOCK * BLOCK * HEAD,
            bytes_accessed=16 << 20,
            transcendentals=0,
        ),
        name="backward",
    )(links, rows, grads, attended, weights, sink_weight)


def pack_kernel(*refs):
    *sources, out = refs
    tokens = sources[0].shape[1]
    for part, source in enumerate(sources):
        for h in range(out.shape[0]):
            out[h, pl.ds(part * tokens, tokens), :] = source[0, :, pl.ds(h * HEAD, HEAD)]


def unpack_kernel(source, *outs):
    tokens = outs[0].shape[1]
    for part, out in enumerate(outs):
        for h in range(source.shape[0]):
            out[0, :, pl.ds(h * HEAD, HEAD)] = source[h, pl.ds(part * tokens, tokens), :]


def relayout_specs(tokens, count, group):
    flat = pl.BlockSpec((1, tokens, group * HEAD), lambda i: (0, 0, i))
    split = pl.BlockSpec((group, count * tokens, HEAD), lambda i: (i, 0, 0))
    return flat, split


def pack(*arrays, group=4):
    _, tokens, columns = arrays[0].shape
    heads = columns // HEAD
    count = len(arrays)
    flat, split = relayout_specs(tokens, count, group)
    return pl.pallas_call(
        pack_kernel,
        grid=(heads // group,),
        out_shape=jax.ShapeDtypeStruct((heads, count * tokens, HEAD), arrays[0].dtype),
        in_specs=[flat] * count,
        out_specs=split,
        cost_estimate=pl.CostEstimate(
            flops=0, bytes_accessed=4 * count * tokens * columns, transcendentals=0),
        name="pack",
    )(*arrays)


def unpack(array, count, group=4):
    heads, depth, _ = array.shape
    tokens = depth // count
    flat, split = relayout_specs(tokens, count, group)
    return pl.pallas_call(
        unpack_kernel,
        grid=(heads // group,),
        out_shape=(jax.ShapeDtypeStruct((1, tokens, heads * HEAD), array.dtype),) * count,
        in_specs=[split],
        out_specs=(flat,) * count,
        cost_estimate=pl.CostEstimate(
            flops=0, bytes_accessed=4 * heads * depth * HEAD, transcendentals=0),
        name="unpack",
    )(array)


def exchange(array):
    return lax.all_to_all(array, "seq", split_axis=0, concat_axis=0, tiled=True)


def sum_everywhere(values):
    for axis in ("dp", "seq"):
        size = lax.axis_size(axis)
        step = 1
        while step < size:
            pairs = [(i, i ^ step) for i in range(size)]
            values = values + lax.ppermute(values, axis, pairs)
            step *= 2
    return values


def on_device(query_rows, key_rows, value_rows, sink_logit, grad_out, pattern):
    heads, blocks, slots = pattern.shape
    head = lax.axis_index("seq")
    links = lax.dynamic_index_in_dim(pattern, head, 0, keepdims=False).reshape(blocks * slots)
    sink = lax.dynamic_slice_in_dim(sink_logit, head, 1, 0)
    scaling = HEAD ** -0.5

    rows = exchange(pack(query_rows, key_rows, value_rows))
    grads = exchange(pack(grad_out))
    attended, weights, sink_weight = forward(links, sink, rows, scaling, slots)
    attended_tokens = exchange(attended)
    gradients, sink_terms = backward(
        links, rows, grads, attended, weights, sink_weight, scaling, slots)
    gradient_tokens = exchange(gradients)

    own = (lax.broadcasted_iota(jnp.int32, (heads,), 0) == head).astype(F32)
    grad_sink = sum_everywhere(own * -jnp.sum(sink_terms[0])) / lax.axis_size("dp")
    grad_query, grad_key, grad_value = unpack(gradient_tokens, 3)
    (out,) = unpack(attended_tokens, 1)
    return out, grad_query, grad_key, grad_value, grad_sink


def solution(mesh):
    placed = (
        P("dp", "seq", None),
        P("dp", "seq", None),
        P("dp", "seq", None),
        P(),
        P("dp", "seq", None),
        P(),
    )
    return jax.shard_map(
        on_device,
        mesh=mesh,
        in_specs=placed,
        out_specs=(
            P("dp", "seq", None),
            P("dp", "seq", None),
            P("dp", "seq", None),
            P("dp", "seq", None),
            P(),
        ),
        check_vma=False,
    )
```

time: 542 us -> 201 us (0.37); the launches traced: 534 us -> 200 us
  other arithmetic: 154 us -> 1.14 us
  matrix products: 103 us -> 0 us
  local copies, waits for them, and re-layouts: 88.2 us -> 7.88 us
  blocking collectives: 77.3 us -> 0 us
  Pallas kernels: 0 us -> 74 us
  waiting for transfers between devices: 63.5 us -> 72.2 us
  loops' own time: 5.86 us -> 0 us
    scatter-add x16 -> x0, other arithmetic: 112 us -> none  [the longest x8 56.1 us: backward_one_group(): key_acc = key_acc.at[flat_links].add(key_part.reshape(-1, BLOCK, HEAD))]
    dot_general x56 -> x0, matrix products: 103 us -> none  [the longest x16 25.5 us: tile_scores(): jnp.einsum('gqe,gkbe->gqkb', queries, key_tiles, preferred_element_type=j...]
    psum x1 -> x0, blocking collectives: 77.3 us -> none  [on_device(): summed = lax.psum(spread, ('seq', 'dp'))]
    pallas_call x0 -> x6, Pallas kernels: none -> 74 us  [the longest x1 30.7 us: backward(): pl.pallas_call(functools.partial(backward_kernel, blocks, slots, per_devi...]
    gather x32 -> x0, local copies, waits for them, and re-layouts: 38.4 us -> none  [the longest x8 13.2 us: backward_one_group(): value_tiles = value_all[chosen]]
    ppermute x0 -> x8, waiting for transfers between devices: none -> 33.2 us  [sum_everywhere(): values = values + lax.ppermute(values, axis, pairs)]
    all_to_all x8 -> x4, waiting for transfers between devices: 63.5 us -> 39 us  [exchange(): return lax.all_to_all(array, 'seq', split_axis=0, concat_axis=0, tiled=True)]
    unnamed x36 -> x12, local copies, waits for them, and re-layouts: 30.9 us -> 7.13 us
  transfers between devices with their start and end apart: 8 -> 12, of which waited for: 5 -> 9; matrix products, arithmetic and copies ran while one was open for 64% -> 1% of each run, Pallas kernels for 0% -> 33%
where the time goes in v1:
time: 201 us; the launch traced here: 200 us
  Pallas kernels  74 us (37%)
  waiting for transfers between devices  72.2 us (36%)
  starting transfers between devices  43.1 us (21%)
  local copies, waits for them, and re-layouts  7.88 us (4%)
    all_to_all x4, waiting for transfers between devices, exchange(): return lax.all_to_all(array, 'seq', split_axis=0, concat_axis=0, tiled=True)  39 us
    ppermute x8, waiting for transfers between devices, sum_everywhere(): values = values + lax.ppermute(values, axis, pairs)  33.2 us
    pallas_call x1, Pallas kernels, backward(): pl.pallas_call(functools.partial(backward_kernel, blocks, slots, per_devi...  30.7 us
    all_to_all x4, starting transfers between devices, exchange(): return lax.all_to_all(array, 'seq', split_axis=0, concat_axis=0, tiled=True)  29.3 us
    pallas_call x1, Pallas kernels, forward(): pl.pallas_call(functools.partial(forward_kernel, blocks, slots, per_devic...  27.7 us
    ppermute x8, starting transfers between devices, sum_everywhere(): values = values + lax.ppermute(values, axis, pairs)  13.8 us
    pallas_call x2, Pallas kernels, pack(): pl.pallas_call(pack_kernel, grid=(heads // group,), out_shape=jax.ShapeDt...  7.8 us
    pallas_call x2, Pallas kernels, unpack(): pl.pallas_call(unpack_kernel, grid=(heads // group,), out_shape=(jax.Shap...  7.76 us
  transfers between devices with their start and end apart: 12, of which 9 were waited for; matrix products, arithmetic and copies ran while one was open for 1% of the time, Pallas kernels for 33%

profile of v1, /device:TPU:64, one launch (start us, length us, event | category | flops | bytes accessed | tf_op | source)
XLA Modules:
  0.0 199.7 jit_solution(12489945990505305080)
XLA Ops:
  0.6 4.4 %pack.2 = bf16[16,768,128]{2,1,0:T(8,128)(2,1)} custom-call(bf16[1,256,2048]{2,1,0:T(8,128)(2,1)} %refs_0_.2, bf16[1,256,2048]{2,1,0:T(8,128)(2,1)} %refs_1_.1, bf16[1,256,2048]{2,1,0:T(8,128)(2,1)} %refs_2_.1), custom_call_target="tpu_custom_call" | custom-call | bytes 6291456 | tf_op jit(solution)/shard_map/pack/pallas_call | solution.py:196
  5.0 7.0 %all-to-all-start = ((bf16[16,768,128]{2,1,0:T(8,128)(2,1)}), bf16[16,768,128]{2,1,0:T(8,128)(2,1)S(1)}, u32[]{:S(2)}, u32[]{:S(2)}) async-start(bf16[16,768,128]{2,1,0:T(8,128)(2,1)} %pack.2), calls=%async_computation | async-start | bytes 6291456 | tf_op jit(solution)/shard_map/all_to_all | solution.py:225
  12.1 3.4 %pack.3 = bf16[16,256,128]{2,1,0:T(8,128)(2,1)} custom-call(bf16[1,256,2048]{2,1,0:T(8,128)(2,1)} %refs_0_.3), custom_call_target="tpu_custom_call" | custom-call | bytes 2097152 | tf_op jit(solution)/shard_map/pack/pallas_call | solution.py:196
  15.5 39.0 %all-to-all-done.rows = bf16[16,768,128]{2,1,0:T(8,128)(2,1)S(1)} async-done(((bf16[16,768,128]{2,1,0:T(8,128)(2,1)}), bf16[16,768,128]{2,1,0:T(8,128)(2,1)S(1)}, u32[]{:S(2)}, u32[]{:S(2)}) %all-to-all-start) | async-done | bytes 3145760 | tf_op jit(solution)/shard_map/all_to_all | solution.py:225
  54.5 7.9 %all-to-all-start.2 = ((bf16[16,256,128]{2,1,0:T(8,128)(2,1)}), bf16[16,256,128]{2,1,0:T(8,128)(2,1)}, u32[]{:S(2)}, u32[]{:S(2)}) async-start(bf16[16,256,128]{2,1,0:T(8,128)(2,1)} %pack.3), calls=%async_computation.2 | async-start | bytes 2097152 | tf_op jit(solution)/shard_map/all_to_all | solution.py:225
  62.5 0.6 dynamic_slice.8.sink
  63.2 27.7 %forward.1 = (bf16[16,256,128]{2,1,0:T(8,128)(2,1)S(1)}, bf16[32,1024,128]{2,1,0:T(8,128)(2,1)S(1)}, f32[32,128]{1,0:T(8,128)S(1)}) custom-call(s32[256]{0:T(256)S(1)} %reshape.14.links, f32[1]{0:T(128)} %dynamic_slice.8.sink, bf16[16,768,128]{2,1,0:T(8,128)(2,1)S(1)} %all-to-all-done.rows), custom_call_target="tpu_custom_call" | custom-call | flops 2147483648 | bytes 14680064 | tf_op jit(solution)/shard_map/forward/pallas_call | solution.py:119
  90.9 1.0 copy-done.1
  91.9 3.3 %copy-done.3 = bf16[32,1024,128]{2,1,0:T(8,128)(2,1)} copy-done((bf16[32,1024,128]{2,1,0:T(8,128)(2,1)}, bf16[32,1024,128]{2,1,0:T(8,128)(2,1)S(1)}, u32[]{:S(2)}) %copy-start.3) | copy-done | bytes 8388632
  95.2 7.2 %all-to-all-start.1 = ((bf16[16,256,128]{2,1,0:T(8,128)(2,1)}), bf16[16,256,128]{2,1,0:T(8,128)(2,1)}, u32[]{:S(2)}, u32[]{:S(2)}) async-start(bf16[16,256,128]{2,1,0:T(8,128)(2,1)} %copy-done.1), calls=%async_computation.1 | async-start | bytes 2097152 | tf_op jit(solution)/shard_map/all_to_all | solution.py:225
  102.4 1.2 copy-done.2
  103.6 30.7 %backward.1 = (bf16[16,768,128]{2,1,0:T(8,128)(2,1)}, f32[8,128]{1,0:T(8,128)S(1)}) custom-call(s32[256]{0:T(256)S(1)} %reshape.14.links, bf16[16,768,128]{2,1,0:T(8,128)(2,1)S(1)} %all-to-all-done.rows, bf16[16,256,128]{2,1,0:T(8,128)(2,1)} %all-to-all-done.2.grads, bf16[16,256,128]{2,1,0:T(8,128)(2,1)S(1)} %copy-done.2, bf16[32,1024,128]{2,1,0:T(8,128)(2,1)} %copy-done.3, ...), custom_call_target="tpu_custom_call" | custom-call | flops 4294967296 | bytes 16777216 | tf_op jit(solution)/shard_map/backward/pallas_call | solution.py:146
  134.3 7.2 %all-to-all-start.3 = ((bf16[16,768,128]{2,1,0:T(8,128)(2,1)}), bf16[16,768,128]{2,1,0:T(8,128)(2,1)S(1)}, u32[]{:S(2)}, u32[]{:S(2)}) async-start(bf16[16,768,128]{2,1,0:T(8,128)(2,1)} %get-tuple-element.16), calls=%async_computation.3 | async-start | bytes 6291456 | tf_op jit(solution)/shard_map/all_to_all | solution.py:225
  141.5 0.6 slice_reduce_fusion
  142.8 0.1 collective-permute-start
  142.9 1.1 collective-permute-done
  144.0 1.9 collective-permute-start.1
  145.9 1.6 collective-permute-done.1
  147.6 4.4 %collective-permute-done.2 = f32[16]{0:T(128)S(1)} collective-permute-done((f32[16]{0:T(128)S(1)}, f32[16]{0:T(128)S(1)}, u32[]{:S(2)}, u32[]{:S(2)}) %collective-permute-start.2) | collective-permute-done | bytes 96 | tf_op jit(solution)/shard_map/ppermute | solution.py:234
  152.0 5.4 %collective-permute-start.3 = (f32[16]{0:T(128)S(1)}, f32[16]{0:T(128)S(1)}, u32[]{:S(2)}, u32[]{:S(2)}) collective-permute-start(f32[16]{0:T(128)S(1)} %add.32), channel_id=1, source_target_pairs={{0,8},{1,9},{2,10},{3,11},{4,12},{5,13},{6,14},{7,15},{8,0},{9,1},... | collective-permute-start | bytes 200 | tf_op jit(solution)/shard_map/ppermute | solution.py:234
  157.4 2.0 %collective-permute-done.3 = f32[16]{0:T(128)S(1)} collective-permute-done((f32[16]{0:T(128)S(1)}, f32[16]{0:T(128)S(1)}, u32[]{:S(2)}, u32[]{:S(2)}) %collective-permute-start.3) | collective-permute-done | bytes 96 | tf_op jit(solution)/shard_map/ppermute | solution.py:234
  159.4 1.9 collective-permute-start.4
  161.4 11.0 %collective-permute-done.4 = f32[16]{0:T(128)S(1)} collective-permute-done((f32[16]{0:T(128)S(1)}, f32[16]{0:T(128)S(1)}, u32[]{:S(2)}, u32[]{:S(2)}) %collective-permute-start.4) | collective-permute-done | bytes 96 | tf_op jit(solution)/shard_map/ppermute | solution.py:234
  172.4 8.2 %collective-permute-done.5 = f32[16]{0:T(128)S(1)} collective-permute-done((f32[16]{0:T(128)S(1)}, f32[16]{0:T(128)S(1)}, u32[]{:S(2)}, u32[]{:S(2)}) %collective-permute-start.5) | collective-permute-done | bytes 96 | tf_op jit(solution)/shard_map/ppermute | solution.py:234
  180.6 2.6 %collective-permute-start.6 = (f32[16]{0:T(128)S(1)}, f32[16]{0:T(128)S(1)}, u32[]{:S(2)}, u32[]{:S(2)}) collective-permute-start(f32[16]{0:T(128)S(1)} %add.35), channel_id=1, source_target_pairs={{0,64},{16,80},{32,96},{48,112},{64,0},{80,16},{96,32},{112,48},{1... | collective-permute-start | bytes 200 | tf_op jit(solution)/shard_map/ppermute | solution.py:234
  183.2 1.5 collective-permute-done.6
  184.7 1.9 collective-permute-start.7
  186.6 3.2 %collective-permute-done.7 = f32[16]{0:T(128)S(1)} collective-permute-done((f32[16]{0:T(128)S(1)}, f32[16]{0:T(128)S(1)}, u32[]{:S(2)}, u32[]{:S(2)}) %collective-permute-start.7) | collective-permute-done | bytes 96 | tf_op jit(solution)/shard_map/ppermute | solution.py:234
  189.8 0.5 add_multiply_fusion
  190.3 3.4 %unpack.2 = bf16[1,256,2048]{2,1,0:T(8,128)(2,1)} custom-call(bf16[16,256,128]{2,1,0:T(8,128)(2,1)} %all-to-all-done.1.source), custom_call_target="tpu_custom_call" | custom-call | bytes 2097152 | tf_op jit(solution)/shard_map/unpack/pallas_call | solution.py:212
  193.7 1.6 copy-done.4
  195.4 4.3 %unpack.3 = (bf16[1,256,2048]{2,1,0:T(8,128)(2,1)}, bf16[1,256,2048]{2,1,0:T(8,128)(2,1)}, bf16[1,256,2048]{2,1,0:T(8,128)(2,1)}) custom-call(bf16[16,768,128]{2,1,0:T(8,128)(2,1)} %copy-done.4), custom_call_target="tpu_custom_call" | custom-call | bytes 6291456 | tf_op jit(solution)/shard_map/unpack/pallas_call | solution.py:212
  (24 shorter events, 0.2 us)
Async XLA Ops:
  0.6 62.4 %copy-start = (s32[16,32,8]{1,2,0:T(8,128)S(1)}, s32[16,32,8]{1,2,0:T(8,128)}, u32[]{:S(2)}) copy-start(s32[16,32,8]{1,2,0:T(8,128)} %param.11) | copy-start | bytes 49156
  5.0 49.5 %all-to-all-start = ((bf16[16,768,128]{2,1,0:T(8,128)(2,1)}), bf16[16,768,128]{2,1,0:T(8,128)(2,1)S(1)}, u32[]{:S(2)}, u32[]{:S(2)}) async-start(bf16[16,768,128]{2,1,0:T(8,128)(2,1)} %pack.2), calls=%async_computation | async-start | bytes 6291456 | tf_op jit(solution)/shard_map/all_to_all | solution.py:225
  12.1 50.4 %copy-start.5 = (f32[16]{0:T(128)S(1)}, f32[16]{0:T(128)}, u32[]{:S(2)}) copy-start(f32[16]{0:T(128)} %param.9) | copy-start | bytes 196
  54.5 40.6 %all-to-all-start.2 = ((bf16[16,256,128]{2,1,0:T(8,128)(2,1)}), bf16[16,256,128]{2,1,0:T(8,128)(2,1)}, u32[]{:S(2)}, u32[]{:S(2)}) async-start(bf16[16,256,128]{2,1,0:T(8,128)(2,1)} %pack.3), calls=%async_computation.2 | async-start | bytes 2097152 | tf_op jit(solution)/shard_map/all_to_all | solution.py:225
  90.9 1.0 copy-start.1
  91.9 3.3 %copy-start.3 = (bf16[32,1024,128]{2,1,0:T(8,128)(2,1)}, bf16[32,1024,128]{2,1,0:T(8,128)(2,1)S(1)}, u32[]{:S(2)}) copy-start(bf16[32,1024,128]{2,1,0:T(8,128)(2,1)S(1)} %get-tuple-element.14.weights) | copy-start | bytes 25165828
  95.2 39.2 %all-to-all-start.1 = ((bf16[16,256,128]{2,1,0:T(8,128)(2,1)}), bf16[16,256,128]{2,1,0:T(8,128)(2,1)}, u32[]{:S(2)}, u32[]{:S(2)}) async-start(bf16[16,256,128]{2,1,0:T(8,128)(2,1)} %copy-done.1), calls=%async_computation.1 | async-start | bytes 2097152 | tf_op jit(solution)/shard_map/all_to_all | solution.py:225
  102.4 1.3 copy-start.2
  134.3 59.4 %all-to-all-start.3 = ((bf16[16,768,128]{2,1,0:T(8,128)(2,1)}), bf16[16,768,128]{2,1,0:T(8,128)(2,1)S(1)}, u32[]{:S(2)}, u32[]{:S(2)}) async-start(bf16[16,768,128]{2,1,0:T(8,128)(2,1)} %get-tuple-element.16), calls=%async_computation.3 | async-start | bytes 6291456 | tf_op jit(solution)/shard_map/all_to_all | solution.py:225
  142.8 1.2 collective-permute-start
  144.0 3.5 %collective-permute-start.1 = (f32[16]{0:T(128)S(1)}, f32[16]{0:T(128)S(1)}, u32[]{:S(2)}, u32[]{:S(2)}) collective-permute-start(f32[16]{0:T(128)S(1)} %fusion), channel_id=1, source_target_pairs={{0,2},{1,3},{2,0},{3,1},{4,6},{5,7},{6,4},{7,5},{8,10},{9,11},{10,... | collective-permute-start | bytes 200 | tf_op jit(solution)/shard_map/ppermute | solution.py:234
  147.5 4.4 %collective-permute-start.2 = (f32[16]{0:T(128)S(1)}, f32[16]{0:T(128)S(1)}, u32[]{:S(2)}, u32[]{:S(2)}) collective-permute-start(f32[16]{0:T(128)S(1)} %fusion.1), channel_id=1, source_target_pairs={{0,4},{1,5},{2,6},{3,7},{4,0},{5,1},{6,2},{7,3},{8,12},{9,13},{10,... | collective-permute-start | bytes 200 | tf_op jit(solution)/shard_map/ppermute | solution.py:234
  152.0 7.4 %collective-permute-start.3 = (f32[16]{0:T(128)S(1)}, f32[16]{0:T(128)S(1)}, u32[]{:S(2)}, u32[]{:S(2)}) collective-permute-start(f32[16]{0:T(128)S(1)} %add.32), channel_id=1, source_target_pairs={{0,8},{1,9},{2,10},{3,11},{4,12},{5,13},{6,14},{7,15},{8,0},{9,1},... | collective-permute-start | bytes 200 | tf_op jit(solution)/shard_map/ppermute | solution.py:234
  159.4 12.9 %collective-permute-start.4 = (f32[16]{0:T(128)S(1)}, f32[16]{0:T(128)S(1)}, u32[]{:S(2)}, u32[]{:S(2)}) collective-permute-start(f32[16]{0:T(128)S(1)} %add.33), channel_id=1, source_target_pairs={{0,16},{16,0},{32,48},{48,32},{64,80},{80,64},{96,112},{112,96},{1... | collective-permute-start | bytes 200 | tf_op jit(solution)/shard_map/ppermute | solution.py:234
  172.4 8.3 %collective-permute-start.5 = (f32[16]{0:T(128)S(1)}, f32[16]{0:T(128)S(1)}, u32[]{:S(2)}, u32[]{:S(2)}) collective-permute-start(f32[16]{0:T(128)S(1)} %add.34), channel_id=1, source_target_pairs={{0,32},{16,48},{32,0},{48,16},{64,96},{80,112},{96,64},{112,80},{1... | collective-permute-start | bytes 200 | tf_op jit(solution)/shard_map/ppermute | solution.py:234
  180.6 4.1 %collective-permute-start.6 = (f32[16]{0:T(128)S(1)}, f32[16]{0:T(128)S(1)}, u32[]{:S(2)}, u32[]{:S(2)}) collective-permute-start(f32[16]{0:T(128)S(1)} %add.35), channel_id=1, source_target_pairs={{0,64},{16,80},{32,96},{48,112},{64,0},{80,16},{96,32},{112,48},{1... | collective-permute-start | bytes 200 | tf_op jit(solution)/shard_map/ppermute | solution.py:234
  184.7 5.0 %collective-permute-start.7 = (f32[16]{0:T(128)S(1)}, f32[16]{0:T(128)S(1)}, u32[]{:S(2)}, u32[]{:S(2)}) collective-permute-start(f32[16]{0:T(128)S(1)} %add.36), channel_id=1, source_target_pairs={{0,128},{16,144},{32,160},{48,176},{64,192},{80,208},{96,224},{112... | collective-permute-start | bytes 200 | tf_op jit(solution)/shard_map/ppermute | solution.py:234
  193.7 1.6 copy-start.4

commit v2 on v1

v2 whole, which is shorter than its diff:
```python
import functools

import jax
import jax.numpy as jnp
from jax import lax
from jax.experimental import pallas as pl
from jax.experimental.pallas import tpu as pltpu
from jax.sharding import PartitionSpec as P

HEAD = 128
BLOCK = 128
LOG2E = 1.4426950408889634
EXTRA = 16
VMEM_GRANT = 60 << 20
F32 = jnp.float32
BF16 = jnp.bfloat16

NT = (((1,), (1,)), ((), ()))
NN = (((1,), (0,)), ((), ()))
TN = (((0,), (0,)), ((), ()))
VMEM_WHOLE = pl.BlockSpec(memory_space=pltpu.VMEM)
SMEM_WHOLE = pl.BlockSpec(memory_space=pltpu.SMEM)
IN_PLACE = pl.BlockSpec(memory_space=pl.ANY)


def dot(left, right, dims):
    return lax.dot_general(left, right, dims, preferred_element_type=F32)


def tile(ref, block, part, per_device):
    rows = per_device * BLOCK
    half = lax.rem(block, per_device)
    start = pl.multiple_of(part * rows + half * BLOCK, BLOCK)
    return ref.at[lax.div(block, per_device), pl.ds(start, BLOCK), :]


def forward_kernel(blocks, slots, per_device, scaling, links, sink, rows, out, weights, sink_weight,
                   score, weight, result, weight_sem, result_sem):
    sink_value = sink[0]
    chunks = weight_sem.shape[0]
    chunk = blocks // chunks

    def send_weight(i):
        span = pl.ds(i * chunk, chunk)
        return pltpu.make_async_copy(weight.at[span], weights.at[span], weight_sem.at[i])

    def scores_of(b, held):
        queries = tile(rows, b, 0, per_device)[...]
        top = None
        for j in range(slots):
            keys = tile(rows, links[b * slots + j], 1, per_device)[...]
            part = dot(keys, queries, NT)
            held[pl.ds(j * BLOCK, BLOCK), :] = part
            part_top = jnp.max(part, axis=0, keepdims=True)
            top = part_top if top is None else jnp.maximum(top, part_top)
        return jnp.maximum(top * scaling, sink_value)

    def attend(b):
        values = jnp.concatenate(
            [tile(rows, links[b * slots + j], 2, per_device)[...] for j in range(slots)], axis=0)
        tile(result, b, 0, per_device)[...] = dot(weight[b], values, TN).astype(BF16)

    def softmax(b, top, held):
        shift = top * LOG2E
        sink_part = jnp.exp(sink_value - top)
        total = sink_part
        for j in range(slots):
            part = jnp.exp2(held[pl.ds(j * BLOCK, BLOCK), :] * (scaling * LOG2E) - shift)
            held[pl.ds(j * BLOCK, BLOCK), :] = part
            total = total + jnp.sum(part, axis=0, keepdims=True)
        inverse = 1.0 / total
        for j in range(slots):
            weight[b, pl.ds(j * BLOCK, BLOCK), :] = (
                held[pl.ds(j * BLOCK, BLOCK), :] * inverse).astype(BF16)
        sink_weight[pl.ds(b, 1), :] = sink_part * inverse

    def step(b, top, u):
        top_next = scores_of(jnp.minimum(b + 1, blocks - 1), score.at[1 - u])
        attend(jnp.maximum(b - 1, 0))
        softmax(b, top, score.at[u])
        return top_next

    def pair(i, top):
        return step(2 * i + 1, step(2 * i, top, 0), 1)

    def one_chunk(i, top):
        half = chunk // 2
        top = lax.fori_loop(i * half, (i + 1) * half, pair, top)
        send_weight(i).start()
        return top

    weight[0] = jnp.zeros(weight.shape[1:], BF16)
    lax.fori_loop(0, chunks, one_chunk, scores_of(0, score.at[0]))
    attend(blocks - 1)
    send_result = pltpu.make_async_copy(result, out.at[:, pl.ds(0, result.shape[1]), :], result_sem)
    send_result.start()
    for i in range(chunks):
        send_weight(i).wait()
    send_result.wait()


def row_dot_kernel(blocks, per_device, grads_in, attended_in, sink_weight, out, row_dot, grads,
                   attended, terms, load_sem, send_sem):
    tokens = grads.shape[1]
    own = attended_in.at[:, pl.ds(0, tokens), :]
    loads = [
        pltpu.make_async_copy(grads_in, grads, load_sem.at[0]),
        pltpu.make_async_copy(own, attended, load_sem.at[1]),
    ]
    for load in loads:
        load.start()
    for load in loads:
        load.wait()

    def one_block(b, carry):
        grad = tile(grads, b, 0, per_device)[...].astype(F32)
        product = grad * tile(attended, b, 0, per_device)[...].astype(F32)
        row_dot[pl.ds(b, 1), :] = jnp.sum(product.T, axis=0, keepdims=True)
        return carry

    lax.fori_loop(0, blocks, one_block, 0, unroll=4)
    rest = -jnp.sum(sink_weight[...] * row_dot[...], keepdims=True)
    row = lax.broadcasted_iota(jnp.int32, terms.shape[1:], 0)
    stacked = jnp.zeros(terms.shape[1:], F32)
    for i in range(3):
        addend = rest.astype(BF16).astype(F32)
        stacked = jnp.where(row == i, addend, stacked)
        rest = rest - addend
    terms[...] = jnp.broadcast_to(stacked.astype(BF16)[None], terms.shape)
    send = pltpu.make_async_copy(
        terms, out.at[:, pl.ds(tokens, terms.shape[1]), :], send_sem)
    send.start()
    send.wait()


def backward_kernel(blocks, slots, per_device, scaling, links, rows, grads_in, weights, row_dot,
                    out, change, key_sum, value_sum, grads, weight, ready, weight_sem, load_sem,
                    send_sem):
    load = pltpu.make_async_copy(grads_in, grads, load_sem)
    load.start()
    chunks = weight_sem.shape[0]
    chunk = blocks // chunks

    def fetch(i):
        span = pl.ds(i * chunk, chunk)
        return pltpu.make_async_copy(weights.at[span], weight.at[span], weight_sem.at[i])

    for i in range(chunks):
        fetch(i).start()

    def prepare(c, carry):
        key_sum[c] = jnp.zeros((BLOCK, HEAD), F32)
        value_sum[c] = jnp.zeros((BLOCK, HEAD), F32)
        return carry

    lax.fori_loop(0, blocks, prepare, 0)
    load.wait()

    def score_grads(b, j, dots, held):
        values = tile(rows, links[b * slots + j], 2, per_device)[...]
        grad_weight = dot(values, tile(grads, b, 0, per_device)[...], NT)
        part = weight[b, pl.ds(j * BLOCK, BLOCK), :].astype(F32)
        held[pl.ds(j * BLOCK, BLOCK), :] = (part * (grad_weight - dots)).astype(BF16)

    def collect(b, j, held):
        c = links[b * slots + j]
        value_sum[c] += dot(
            weight[b, pl.ds(j * BLOCK, BLOCK), :], tile(grads, b, 0, per_device)[...], NN)
        key_sum[c] += dot(
            held[pl.ds(j * BLOCK, BLOCK), :], tile(rows, b, 0, per_device)[...], NN)

    def query_grad(b, held):
        keys = jnp.concatenate(
            [tile(rows, links[b * slots + j], 1, per_device)[...] for j in range(slots)], axis=0)
        tile(ready, b, 0, per_device)[...] = (dot(held[...], keys, TN) * scaling).astype(BF16)

    def step(b, u):
        ahead = jnp.minimum(b + 1, blocks - 1)
        dots = row_dot[pl.ds(ahead, 1), :]
        for j in range(slots):
            score_grads(ahead, j, dots, change.at[1 - u])
            collect(b, j, change.at[u])
        query_grad(b, change.at[u])

    def pair(i, carry):
        step(2 * i, 0)
        step(2 * i + 1, 1)
        return carry

    fetch(0).wait()
    for j in range(slots):
        score_grads(0, j, row_dot[pl.ds(0, 1), :], change.at[0])

    def one_chunk(i, carry):
        @pl.when(i + 1 < chunks)
        def _():
            fetch(i + 1).wait()

        half = chunk // 2
        return lax.fori_loop(i * half, (i + 1) * half, pair, carry)

    lax.fori_loop(0, chunks, one_chunk, 0)

    def finish(c, carry):
        tile(ready, c, 1, per_device)[...] = (key_sum[c] * scaling).astype(BF16)
        tile(ready, c, 2, per_device)[...] = value_sum[c].astype(BF16)
        return carry

    lax.fori_loop(0, blocks, finish, 0, unroll=2)
    send = pltpu.make_async_copy(ready, out, send_sem)
    send.start()
    send.wait()


def forward(links, sink, rows, scaling, slots):
    peers, depth, _ = rows.shape
    tokens = depth // 3
    per_device = tokens // BLOCK
    blocks = peers * per_device
    return pl.pallas_call(
        functools.partial(forward_kernel, blocks, slots, per_device, scaling),
        out_shape=(
            jax.ShapeDtypeStruct((peers, tokens + EXTRA, HEAD), BF16),
            jax.ShapeDtypeStruct((blocks, slots * BLOCK, BLOCK), BF16),
            jax.ShapeDtypeStruct((blocks, BLOCK), F32),
        ),
        in_specs=[SMEM_WHOLE, SMEM_WHOLE, VMEM_WHOLE],
        out_specs=(IN_PLACE, IN_PLACE, VMEM_WHOLE),
        scratch_shapes=[
            pltpu.VMEM((2, slots * BLOCK, BLOCK), F32),
            pltpu.VMEM((blocks, slots * BLOCK, BLOCK), BF16),
            pltpu.VMEM((peers, tokens, HEAD), BF16),
            pltpu.SemaphoreType.DMA((4,)),
            pltpu.SemaphoreType.DMA,
        ],
        compiler_params=pltpu.CompilerParams(vmem_limit_bytes=VMEM_GRANT),
        cost_estimate=pl.CostEstimate(
            flops=4 * blocks * slots * BLOCK * BLOCK * HEAD,
            bytes_accessed=14 << 20,
            transcendentals=blocks * slots * BLOCK * BLOCK,
        ),
        name="forward",
    )(links, sink, rows)


def row_dots(grads, attended, sink_weight):
    peers, tokens, _ = grads.shape
    per_device = tokens // BLOCK
    blocks = peers * per_device
    return pl.pallas_call(
        functools.partial(row_dot_kernel, blocks, per_device),
        out_shape=(
            jax.ShapeDtypeStruct(attended.shape, BF16),
            jax.ShapeDtypeStruct((blocks, BLOCK), F32),
        ),
        in_specs=[IN_PLACE, IN_PLACE, VMEM_WHOLE],
        out_specs=(IN_PLACE, VMEM_WHOLE),
        scratch_shapes=[
            pltpu.VMEM((peers, tokens, HEAD), BF16),
            pltpu.VMEM((peers, tokens, HEAD), BF16),
            pltpu.VMEM((peers, EXTRA, HEAD), BF16),
            pltpu.SemaphoreType.DMA((2,)),
            pltpu.SemaphoreType.DMA,
        ],
        input_output_aliases={1: 0},
        compiler_params=pltpu.CompilerParams(vmem_limit_bytes=VMEM_GRANT),
        cost_estimate=pl.CostEstimate(
            flops=3 * blocks * BLOCK * HEAD, bytes_accessed=2 << 20, transcendentals=0),
        name="row_dots",
    )(grads, attended, sink_weight)


def backward(links, rows, grads, weights, row_dot, scaling, slots):
    peers, tokens, _ = grads.shape
    per_device = tokens // BLOCK
    blocks = peers * per_device
    return pl.pallas_call(
        functools.partial(backward_kernel, blocks, slots, per_device, scaling),
        out_shape=jax.ShapeDtypeStruct((peers, 3 * tokens, HEAD), BF16),
        in_specs=[SMEM_WHOLE, VMEM_WHOLE, IN_PLACE, IN_PLACE, VMEM_WHOLE],
        out_specs=IN_PLACE,
        scratch_shapes=[
            pltpu.VMEM((2, slots * BLOCK, BLOCK), BF16),
            pltpu.VMEM((blocks, BLOCK, HEAD), F32),
            pltpu.VMEM((blocks, BLOCK, HEAD), F32),
            pltpu.VMEM((peers, tokens, HEAD), BF16),
            pltpu.VMEM((blocks, slots * BLOCK, BLOCK), BF16),
            pltpu.VMEM((peers, 3 * tokens, HEAD), BF16),
            pltpu.SemaphoreType.DMA((4,)),
            pltpu.SemaphoreType.DMA,
            pltpu.SemaphoreType.DMA,
        ],
        compiler_params=pltpu.CompilerParams(vmem_limit_bytes=VMEM_GRANT),
        cost_estimate=pl.CostEstimate(
            flops=8 * blocks * slots * BLOCK * BLOCK * HEAD,
            bytes_accessed=16 << 20,
            transcendentals=0,
        ),
        name="backward",
    )(links, rows, grads, weights, row_dot)


def pack_kernel(*refs):
    *sources, out, flat, split, load_sem, send_sem = refs
    heads, tokens = split.shape[1], split.shape[2]
    loads, sends = [], []
    for part, source in enumerate(sources):
        loads.append(pltpu.make_async_copy(source.at[0], flat.at[part], load_sem.at[part]))
        span = out.at[:, pl.ds(part * tokens, tokens), :]
        sends.append(pltpu.make_async_copy(split.at[part], span, send_sem.at[part]))
        loads[part].start()
    for part in range(len(sources)):
        loads[part].wait()
        for h in range(heads):
            split[part, h] = flat[part, :, pl.ds(h * HEAD, HEAD)]
        sends[part].start()
    for send in sends:
        send.wait()


def pack(*arrays):
    _, tokens, columns = arrays[0].shape
    heads, count = columns // HEAD, len(arrays)
    return pl.pallas_call(
        pack_kernel,
        out_shape=jax.ShapeDtypeStruct((heads, count * tokens, HEAD), arrays[0].dtype),
        in_specs=[IN_PLACE] * count,
        out_specs=IN_PLACE,
        scratch_shapes=[
            pltpu.VMEM((count, tokens, columns), arrays[0].dtype),
            pltpu.VMEM((count, heads, tokens, HEAD), arrays[0].dtype),
            pltpu.SemaphoreType.DMA((count,)),
            pltpu.SemaphoreType.DMA((count,)),
        ],
        compiler_params=pltpu.CompilerParams(vmem_limit_bytes=VMEM_GRANT),
        cost_estimate=pl.CostEstimate(
            flops=0, bytes_accessed=4 * count * tokens * columns, transcendentals=0),
        name="pack",
    )(*arrays)


def unpack_kernel(source, *refs):
    *outs, flat, send_sem = refs
    heads, tokens = source.shape[0], flat.shape[1]
    sends = []
    for part, out in enumerate(outs):
        for h in range(heads):
            flat[part, :, pl.ds(h * HEAD, HEAD)] = source[h, pl.ds(part * tokens, tokens), :]
        sends.append(pltpu.make_async_copy(flat.at[part], out.at[0], send_sem.at[part]))
        sends[part].start()
    for send in sends:
        send.wait()


def unpack(array, tokens, count, grant):
    heads = array.shape[0]
    return pl.pallas_call(
        unpack_kernel,
        out_shape=(jax.ShapeDtypeStruct((1, tokens, heads * HEAD), array.dtype),) * count,
        in_specs=[VMEM_WHOLE],
        out_specs=(IN_PLACE,) * count,
        scratch_shapes=[
            pltpu.VMEM((count, tokens, heads * HEAD), array.dtype),
            pltpu.SemaphoreType.DMA((count,)),
        ],
        compiler_params=pltpu.CompilerParams(vmem_limit_bytes=grant),
        cost_estimate=pl.CostEstimate(
            flops=0, bytes_accessed=4 * heads * count * tokens * HEAD, transcendentals=0),
        name="unpack",
    )(array)


def exchange(array):
    return lax.all_to_all(array, "seq", split_axis=0, concat_axis=0, tiled=True)


def sum_over_documents(values):
    size = lax.axis_size("dp")
    stride = 1
    while stride < size:
        width = min(4, size // stride)
        shifted = []
        for k in range(1, width):
            pairs = []
            for i in range(size):
                digit = i // stride % width
                pairs.append((i, i + ((digit + k) % width - digit) * stride))
            shifted.append(lax.ppermute(values, "dp", pairs))
        values = functools.reduce(jnp.add, shifted, values)
        stride *= width
    return values


def on_device(query_rows, key_rows, value_rows, sink_logit, grad_out, pattern):
    heads, blocks, slots = pattern.shape
    head = lax.axis_index("seq")
    links = lax.dynamic_index_in_dim(pattern, head, 0, keepdims=False).reshape(blocks * slots)
    sink = lax.dynamic_slice_in_dim(sink_logit, head, 1, 0)
    scaling = HEAD ** -0.5

    tokens = query_rows.shape[1]
    rows = exchange(pack(query_rows, key_rows, value_rows))
    grads = exchange(pack(grad_out))
    attended, weights, sink_weight = forward(links, sink, rows, scaling, slots)
    attended, row_dot = row_dots(grads, attended, sink_weight)
    attended_tokens = exchange(attended)
    gradients = backward(links, rows, grads, weights, row_dot, scaling, slots)
    gradient_tokens = exchange(gradients)

    addends = attended_tokens[:, tokens:tokens + 3, 0].astype(F32)
    grad_sink = sum_over_documents(jnp.sum(addends, axis=1)) / lax.axis_size("dp")
    (out,) = unpack(attended_tokens, tokens, 1, VMEM_GRANT)
    grad_query, grad_key, grad_value = unpack(gradient_tokens, tokens, 3, 8 << 20)
    return out, grad_query, grad_key, grad_value, grad_sink


def solution(mesh):
    placed = (
        P("dp", "seq", None),
        P("dp", "seq", None),
        P("dp", "seq", None),
        P(),
        P("dp", "seq", None),
        P(),
    )
    return jax.shard_map(
        on_device,
        mesh=mesh,
        in_specs=placed,
        out_specs=(
            P("dp", "seq", None),
            P("dp", "seq", None),
            P("dp", "seq", None),
            P("dp", "seq", None),
            P(),
        ),
        check_vma=False,
    )
```

time: 201 us -> 168 us (0.84)
  Pallas kernels: 74 us -> 55.8 us
  waiting for transfers between devices: 72.2 us -> 64 us
  starting transfers between devices: 43.1 us -> 40.2 us
  local copies, waits for them, and re-layouts: 7.88 us -> 5.02 us
    ppermute x8 -> x6, waiting for transfers between devices: 33.2 us -> 2.04 us  [sum_over_documents(): shifted.append(lax.ppermute(values, 'dp', pairs))]
    all_to_all x4, waiting for transfers between devices: 39 us -> 62 us  [exchange(): return lax.all_to_all(array, 'seq', split_axis=0, concat_axis=0, tiled=True)]
    pallas_call x1, Pallas kernels: 27.7 us -> 17.9 us  [forward(): pl.pallas_call(functools.partial(forward_kernel, blocks, slots, per_devic...]
    pallas_call x1, Pallas kernels: 30.7 us -> 22.9 us  [backward(): pl.pallas_call(functools.partial(backward_kernel, blocks, slots, per_devi...]
    unnamed x12 -> x10, local copies, waits for them, and re-layouts: 7.13 us -> 3.7 us
    ppermute x8 -> x6, starting transfers between devices: 13.8 us -> 10.8 us  [sum_over_documents(): shifted.append(lax.ppermute(values, 'dp', pairs))]
    pallas_call x4 -> x5, Pallas kernels: 15.6 us -> 14.9 us  [the longest x2 5.56 us: pack(): pl.pallas_call(pack_kernel, out_shape=jax.ShapeDtypeStruct((heads, count...]
  transfers between devices with their start and end apart: 12 -> 10, of which waited for: 9 -> 4; matrix products, arithmetic and copies ran while one was open for 1% -> 2% of each run, Pallas kernels for 33% -> 27%
where the time goes in v2:
time: 168 us; the launch traced here: 167 us
  waiting for transfers between devices  64 us (38%)
  Pallas kernels  55.8 us (33%)
  starting transfers between devices  40.2 us (24%)
  local copies, waits for them, and re-layouts  5.02 us (3%)
    all_to_all x4, waiting for transfers between devices, exchange(): return lax.all_to_all(array, 'seq', split_axis=0, concat_axis=0, tiled=True)  62 us
    all_to_all x4, starting transfers between devices, exchange(): return lax.all_to_all(array, 'seq', split_axis=0, concat_axis=0, tiled=True)  29.4 us
    pallas_call x1, Pallas kernels, backward(): pl.pallas_call(functools.partial(backward_kernel, blocks, slots, per_devi...  22.9 us
    pallas_call x1, Pallas kernels, forward(): pl.pallas_call(functools.partial(forward_kernel, blocks, slots, per_devic...  17.9 us
    ppermute x6, starting transfers between devices, sum_over_documents(): shifted.append(lax.ppermute(values, 'dp', pairs))  10.8 us
    pallas_call x2, Pallas kernels, pack(): pl.pallas_call(pack_kernel, out_shape=jax.ShapeDtypeStruct((heads, count...  5.56 us
    pallas_call x1, Pallas kernels, row_dots(): pl.pallas_call(functools.partial(row_dot_kernel, blocks, per_device), out...  4.88 us
    pallas_call x2, Pallas kernels, unpack(): pl.pallas_call(unpack_kernel, out_shape=(jax.ShapeDtypeStruct((1, tokens,...  4.49 us
  transfers between devices with their start and end apart: 10, of which 4 were waited for; matrix products, arithmetic and copies ran while one was open for 2% of the time, Pallas kernels for 27%

profile of v2, /device:TPU:64, one launch (start us, length us, event | category | flops | bytes accessed | tf_op | source)
XLA Modules:
  0.0 167.3 jit_solution(4342045171759912167)
XLA Ops:
  0.6 0.0 copy-start
  0.6 3.2 %pack.3 = bf16[16,768,128]{2,1,0:T(8,128)(2,1)} custom-call(bf16[1,256,2048]{2,1,0:T(8,128)(2,1)} %refs_0_.3, bf16[1,256,2048]{2,1,0:T(8,128)(2,1)} %refs_1_.1, bf16[1,256,2048]{2,1,0:T(8,128)(2,1)} %refs_2_.1), custom_call_target="tpu_custom_call" | custom-call | bytes 6291456 | tf_op jit(solution)/shard_map/pack/pallas_call | solution.py:324
  3.8 7.0 %all-to-all-start.1 = ((bf16[16,768,128]{2,1,0:T(8,128)(2,1)}), bf16[16,768,128]{2,1,0:T(8,128)(2,1)S(1)}, u32[]{:S(2)}, u32[]{:S(2)}) async-start(bf16[16,768,128]{2,1,0:T(8,128)(2,1)} %pack.3), calls=%async_computation.1 | async-start | bytes 6291456 | tf_op jit(solution)/shard_map/all_to_all | solution.py:374
  10.9 0.0 copy-start.4
  10.9 2.4 %pack.2 = bf16[16,256,128]{2,1,0:T(8,128)(2,1)} custom-call(bf16[1,256,2048]{2,1,0:T(8,128)(2,1)} %refs_0_.2), custom_call_target="tpu_custom_call" | custom-call | bytes 2097152 | tf_op jit(solution)/shard_map/pack/pallas_call | solution.py:324
  13.3 40.0 %all-to-all-done.1.rows = bf16[16,768,128]{2,1,0:T(8,128)(2,1)S(1)} async-done(((bf16[16,768,128]{2,1,0:T(8,128)(2,1)}), bf16[16,768,128]{2,1,0:T(8,128)(2,1)S(1)}, u32[]{:S(2)}, u32[]{:S(2)}) %all-to-all-start.1) | async-done | bytes 3145760 | tf_op jit(solution)/shard_map/all_to_all | solution.py:374
  53.3 1.7 %copy-done.3 = bf16[16,768,128]{2,1,0:T(8,128)(2,1)} copy-done((bf16[16,768,128]{2,1,0:T(8,128)(2,1)}, bf16[16,768,128]{2,1,0:T(8,128)(2,1)S(1)}, u32[]{:S(2)}) %copy-start.3) | copy-done | bytes 3145752
  55.0 7.9 %all-to-all-start = ((bf16[16,256,128]{2,1,0:T(8,128)(2,1)}), bf16[16,256,128]{2,1,0:T(8,128)(2,1)S(1)}, u32[]{:S(2)}, u32[]{:S(2)}) async-start(bf16[16,256,128]{2,1,0:T(8,128)(2,1)} %pack.2), calls=%async_computation | async-start | bytes 2097152 | tf_op jit(solution)/shard_map/all_to_all | solution.py:374
  62.9 0.6 dynamic_slice.8.sink
  63.5 0.1 copy.12
  63.6 0.7 reshape.15.links
  64.2 17.9 %forward.1 = (bf16[16,272,128]{2,1,0:T(8,128)(2,1)}, bf16[32,1024,128]{2,1,0:T(8,128)(2,1)}, f32[32,128]{1,0:T(8,128)}) custom-call(s32[256]{0:T(256)} %reshape.15.links, f32[1]{0:T(128)} %dynamic_slice.8.sink, bf16[16,768,128]{2,1,0:T(8,128)(2,1)} %copy-done.3), custom_call_target="tpu_custom_call" | custom-call | flops 2147483648 | bytes 14680064 | tf_op jit(solution)/shard_map/forward/pallas_call | solution.py:220
  82.2 0.0 all-to-all-done.grads_in
  82.2 0.0 copy-start.2
  82.2 1.0 copy-done.2
  83.2 4.9 %row_dots.1 = (bf16[16,272,128]{2,1,0:T(8,128)(2,1)}, f32[32,128]{1,0:T(8,128)}) custom-call(bf16[16,256,128]{2,1,0:T(8,128)(2,1)} %copy-done.2, bf16[16,272,128]{2,1,0:T(8,128)(2,1)} %get-tuple-element.13.attended_in, f32[32,128]{1,0:T(8,128)} %get-tuple-element.14.sink_weight), custom_call_target="tpu_custom_call", output_to_operand_aliasing={{0}: (1, {})} | custom-call | flops 1572864 | bytes 2097152 | tf_op jit(solution)/shard_map/row_dots/pallas_call | solution.py:250
  88.1 7.2 %all-to-all-start.2 = ((bf16[16,272,128]{2,1,0:T(8,128)(2,1)}), bf16[16,272,128]{2,1,0:T(8,128)(2,1)S(1)}, u32[]{:S(2)}, u32[]{:S(2)}) async-start(bf16[16,272,128]{2,1,0:T(8,128)(2,1)} %get-tuple-element.15), calls=%async_computation.2 | async-start | bytes 2228224 | tf_op jit(solution)/shard_map/all_to_all | solution.py:374
  95.3 22.9 %backward.1 = bf16[16,768,128]{2,1,0:T(8,128)(2,1)} custom-call(s32[256]{0:T(256)} %reshape.15.links, bf16[16,768,128]{2,1,0:T(8,128)(2,1)} %copy-done.3, bf16[16,256,128]{2,1,0:T(8,128)(2,1)} %copy-done.2, bf16[32,1024,128]{2,1,0:T(8,128)(2,1)} %get-tuple-element.16.weights, f32[32,128]{1,0:T(8,128)} %get-tuple-element.17.row_dot), custom_call_target="tpu_custom_call" | custom-call | flops 4294967296 | bytes 16777216 | tf_op jit(solution)/shard_map/backward/pallas_call | solution.py:277
  118.2 1.0 copy-done.1
  119.2 7.2 %all-to-all-start.3 = ((bf16[16,768,128]{2,1,0:T(8,128)(2,1)}), bf16[16,768,128]{2,1,0:T(8,128)(2,1)S(1)}, u32[]{:S(2)}, u32[]{:S(2)}) async-start(bf16[16,768,128]{2,1,0:T(8,128)(2,1)} %backward.1), calls=%async_computation.3 | async-start | bytes 6291456 | tf_op jit(solution)/shard_map/all_to_all | solution.py:374
  126.4 1.0 convert_reduce_fusion
  127.4 0.1 collective-permute-start.2
  127.5 2.0 %collective-permute-start.1 = (f32[16]{0:T(128)S(1)}, f32[16]{0:T(128)S(1)}, u32[]{:S(2)}, u32[]{:S(2)}) collective-permute-start(f32[16]{0:T(128)S(1)} %convert_reduce_fusion), channel_id=1, source_target_pairs={{0,2},{1,3},{2,0},{3,1},{4,6},{5,7},{6,4},{7,5},{8,10},{9,11},{10,... | collective-permute-start | bytes 200 | tf_op jit(solution)/shard_map/ppermute | solution.py:388
  129.5 0.1 collective-permute-start
  129.7 2.5 %unpack.2 = bf16[1,256,2048]{2,1,0:T(8,128)(2,1)} custom-call(bf16[16,272,128]{2,1,0:T(8,128)(2,1)} %copy-done.1), custom_call_target="tpu_custom_call" | custom-call | bytes 2097152 | tf_op jit(solution)/shard_map/unpack/pallas_call | solution.py:357
  132.2 0.3 collective-permute-done
  132.5 5.9 %collective-permute-start.4 = (f32[16]{0:T(128)S(1)}, f32[16]{0:T(128)S(1)}, u32[]{:S(2)}, u32[]{:S(2)}) collective-permute-start(f32[16]{0:T(128)S(1)} %add_add_fusion), channel_id=1, source_target_pairs={{0,8},{1,9},{2,10},{3,11},{4,12},{5,13},{6,14},{7,15},{8,0},{9,1},... | collective-permute-start | bytes 200 | tf_op jit(solution)/shard_map/ppermute | solution.py:388
  138.4 2.7 %collective-permute-start.3 = (f32[16]{0:T(128)S(1)}, f32[16]{0:T(128)S(1)}, u32[]{:S(2)}, u32[]{:S(2)}) collective-permute-start(f32[16]{0:T(128)S(1)} %add_add_fusion), channel_id=1, source_target_pairs={{0,4},{1,5},{2,6},{3,7},{4,8},{5,9},{6,10},{7,11},{8,12},{9,13},{1... | collective-permute-start | bytes 200 | tf_op jit(solution)/shard_map/ppermute | solution.py:388
  141.1 1.8 %collective-permute-done.3 = f32[16]{0:T(128)S(1)} collective-permute-done((f32[16]{0:T(128)S(1)}, f32[16]{0:T(128)S(1)}, u32[]{:S(2)}, u32[]{:S(2)}) %collective-permute-start.3) | collective-permute-done | bytes 96 | tf_op jit(solution)/shard_map/ppermute | solution.py:388
  142.9 0.5 add_multiply_fusion
  143.4 22.0 %all-to-all-done.3.source = bf16[16,768,128]{2,1,0:T(8,128)(2,1)S(1)} async-done(((bf16[16,768,128]{2,1,0:T(8,128)(2,1)}), bf16[16,768,128]{2,1,0:T(8,128)(2,1)S(1)}, u32[]{:S(2)}, u32[]{:S(2)}) %all-to-all-start.3) | async-done | bytes 3145760 | tf_op jit(solution)/shard_map/all_to_all | solution.py:374
  165.3 2.0 %unpack.3 = (bf16[1,256,2048]{2,1,0:T(8,128)(2,1)}, bf16[1,256,2048]{2,1,0:T(8,128)(2,1)}, bf16[1,256,2048]{2,1,0:T(8,128)(2,1)}) custom-call(bf16[16,768,128]{2,1,0:T(8,128)(2,1)S(1)} %all-to-all-done.3.source), custom_call_target="tpu_custom_call" | custom-call | bytes 6291456 | tf_op jit(solution)/shard_map/unpack/pallas_call | solution.py:357
  (12 shorter events, 0.0 us)
Async XLA Ops:
  0.6 62.9 %copy-start = (s32[16,32,8]{1,2,0:T(8,128)S(1)}, s32[16,32,8]{1,2,0:T(8,128)}, u32[]{:S(2)}) copy-start(s32[16,32,8]{1,2,0:T(8,128)} %param.11) | copy-start | bytes 49156
  3.8 49.5 %all-to-all-start.1 = ((bf16[16,768,128]{2,1,0:T(8,128)(2,1)}), bf16[16,768,128]{2,1,0:T(8,128)(2,1)S(1)}, u32[]{:S(2)}, u32[]{:S(2)}) async-start(bf16[16,768,128]{2,1,0:T(8,128)(2,1)} %pack.3), calls=%async_computation.1 | async-start | bytes 6291456 | tf_op jit(solution)/shard_map/all_to_all | solution.py:374
  10.9 52.0 %copy-start.4 = (f32[16]{0:T(128)S(1)}, f32[16]{0:T(128)}, u32[]{:S(2)}) copy-start(f32[16]{0:T(128)} %param.9) | copy-start | bytes 196
  53.3 1.7 %copy-start.3 = (bf16[16,768,128]{2,1,0:T(8,128)(2,1)}, bf16[16,768,128]{2,1,0:T(8,128)(2,1)S(1)}, u32[]{:S(2)}) copy-start(bf16[16,768,128]{2,1,0:T(8,128)(2,1)S(1)} %all-to-all-done.1.rows) | copy-start | bytes 9437188
  55.0 27.2 %all-to-all-start = ((bf16[16,256,128]{2,1,0:T(8,128)(2,1)}), bf16[16,256,128]{2,1,0:T(8,128)(2,1)S(1)}, u32[]{:S(2)}, u32[]{:S(2)}) async-start(bf16[16,256,128]{2,1,0:T(8,128)(2,1)} %pack.2), calls=%async_computation | async-start | bytes 2097152 | tf_op jit(solution)/shard_map/all_to_all | solution.py:374
  82.2 1.0 copy-start.2
  88.1 30.1 %all-to-all-start.2 = ((bf16[16,272,128]{2,1,0:T(8,128)(2,1)}), bf16[16,272,128]{2,1,0:T(8,128)(2,1)S(1)}, u32[]{:S(2)}, u32[]{:S(2)}) async-start(bf16[16,272,128]{2,1,0:T(8,128)(2,1)} %get-tuple-element.15), calls=%async_computation.2 | async-start | bytes 2228224 | tf_op jit(solution)/shard_map/all_to_all | solution.py:374
  118.2 1.0 copy-start.1
  119.2 46.1 %all-to-all-start.3 = ((bf16[16,768,128]{2,1,0:T(8,128)(2,1)}), bf16[16,768,128]{2,1,0:T(8,128)(2,1)S(1)}, u32[]{:S(2)}, u32[]{:S(2)}) async-start(bf16[16,768,128]{2,1,0:T(8,128)(2,1)} %backward.1), calls=%async_computation.3 | async-start | bytes 6291456 | tf_op jit(solution)/shard_map/all_to_all | solution.py:374
  127.4 4.8 %collective-permute-start.2 = (f32[16]{0:T(128)S(1)}, f32[16]{0:T(128)S(1)}, u32[]{:S(2)}, u32[]{:S(2)}) collective-permute-start(f32[16]{0:T(128)S(1)} %convert_reduce_fusion), channel_id=1, source_target_pairs={{0,3},{1,0},{2,1},{3,2},{4,7},{5,4},{6,5},{7,6},{8,11},{9,8},{10,9... | collective-permute-start | bytes 200 | tf_op jit(solution)/shard_map/ppermute | solution.py:388
  127.5 4.7 %collective-permute-start.1 = (f32[16]{0:T(128)S(1)}, f32[16]{0:T(128)S(1)}, u32[]{:S(2)}, u32[]{:S(2)}) collective-permute-start(f32[16]{0:T(128)S(1)} %convert_reduce_fusion), channel_id=1, source_target_pairs={{0,2},{1,3},{2,0},{3,1},{4,6},{5,7},{6,4},{7,5},{8,10},{9,11},{10,... | collective-permute-start | bytes 200 | tf_op jit(solution)/shard_map/ppermute | solution.py:388
  129.5 3.0 %collective-permute-start = (f32[16]{0:T(128)S(1)}, f32[16]{0:T(128)S(1)}, u32[]{:S(2)}, u32[]{:S(2)}) collective-permute-start(f32[16]{0:T(128)S(1)} %convert_reduce_fusion), channel_id=1, source_target_pairs={{0,1},{1,2},{2,3},{3,0},{4,5},{5,6},{6,7},{7,4},{8,9},{9,10},{10,1... | collective-permute-start | bytes 200 | tf_op jit(solution)/shard_map/ppermute | solution.py:388
  132.5 8.6 %collective-permute-start.5 = (f32[16]{0:T(128)S(1)}, f32[16]{0:T(128)S(1)}, u32[]{:S(2)}, u32[]{:S(2)}) collective-permute-start(f32[16]{0:T(128)S(1)} %add_add_fusion), channel_id=1, source_target_pairs={{0,12},{1,13},{2,14},{3,15},{4,0},{5,1},{6,2},{7,3},{8,4},{9,5},{1... | collective-permute-start | bytes 200 | tf_op jit(solution)/shard_map/ppermute | solution.py:388
  132.5 8.6 %collective-permute-start.4 = (f32[16]{0:T(128)S(1)}, f32[16]{0:T(128)S(1)}, u32[]{:S(2)}, u32[]{:S(2)}) collective-permute-start(f32[16]{0:T(128)S(1)} %add_add_fusion), channel_id=1, source_target_pairs={{0,8},{1,9},{2,10},{3,11},{4,12},{5,13},{6,14},{7,15},{8,0},{9,1},... | collective-permute-start | bytes 200 | tf_op jit(solution)/shard_map/ppermute | solution.py:388
  138.4 4.4 %collective-permute-start.3 = (f32[16]{0:T(128)S(1)}, f32[16]{0:T(128)S(1)}, u32[]{:S(2)}, u32[]{:S(2)}) collective-permute-start(f32[16]{0:T(128)S(1)} %add_add_fusion), channel_id=1, source_target_pairs={{0,4},{1,5},{2,6},{3,7},{4,8},{5,9},{6,10},{7,11},{8,12},{9,13},{1... | collective-permute-start | bytes 200 | tf_op jit(solution)/shard_map/ppermute | solution.py:388

commit v3 on v2

v3 whole, which is shorter than its diff:
```python
import functools

import jax
import jax.numpy as jnp
from jax import lax
from jax.experimental import pallas as pl
from jax.experimental.pallas import tpu as pltpu
from jax.sharding import PartitionSpec as P

HEAD = 128
BLOCK = 128
LOG2E = 1.4426950408889634
EXTRA = 16
VMEM_GRANT = 63 << 20
F32 = jnp.float32
BF16 = jnp.bfloat16

NT = (((1,), (1,)), ((), ()))
NN = (((1,), (0,)), ((), ()))
TN = (((0,), (0,)), ((), ()))
VMEM_WHOLE = pl.BlockSpec(memory_space=pltpu.VMEM)
SMEM_WHOLE = pl.BlockSpec(memory_space=pltpu.SMEM)
IN_PLACE = pl.BlockSpec(memory_space=pl.ANY)


def dot(left, right, dims):
    return lax.dot_general(left, right, dims, preferred_element_type=F32)


def tile(ref, block, part, per_device):
    rows = per_device * BLOCK
    half = lax.rem(block, per_device)
    start = pl.multiple_of(part * rows + half * BLOCK, BLOCK)
    return ref.at[lax.div(block, per_device), pl.ds(start, BLOCK), :]


def forward_kernel(blocks, slots, per_device, scaling, links, sink, rows_in, out, weights,
                   sink_weight, score, rows, weight, result, load_sem, weight_sem, result_sem):
    sink_value = sink[0]
    tokens = result.shape[1]
    loads = []
    for k, span in enumerate((pl.ds(0, 2 * tokens), pl.ds(2 * tokens, tokens))):
        loads.append(pltpu.make_async_copy(
            rows_in.at[:, span, :], rows.at[:, span, :], load_sem.at[k]))
        loads[k].start()
    chunks = weight_sem.shape[0]
    chunk = blocks // chunks
    unroll = score.shape[0]

    def send_weight(i):
        span = pl.ds(i * chunk, chunk)
        return pltpu.make_async_copy(weight.at[span], weights.at[span], weight_sem.at[i])

    def scores_of(b, held):
        queries = tile(rows, b, 0, per_device)[...]
        keys = jnp.concatenate(
            [tile(rows, links[b * slots + j], 1, per_device)[...] for j in range(slots)], axis=0)
        whole = dot(keys, queries, NT)
        held[...] = whole
        top = None
        for j in range(slots):
            part = whole[j * BLOCK:(j + 1) * BLOCK]
            part_top = jnp.max(part.reshape(-1, 8, BLOCK), axis=0)
            top = part_top if top is None else jnp.maximum(top, part_top)
        return jnp.maximum(jnp.max(top, axis=0, keepdims=True) * scaling, sink_value)

    def attend(b):
        values = jnp.concatenate(
            [tile(rows, links[b * slots + j], 2, per_device)[...] for j in range(slots)], axis=0)
        tile(result, b, 0, per_device)[...] = dot(weight[b], values, TN).astype(BF16)

    def softmax(b, top, held):
        shift = top * LOG2E
        sink_part = jnp.exp(sink_value - top)
        total = None
        for j in range(slots):
            part = jnp.exp2(held[pl.ds(j * BLOCK, BLOCK), :] * (scaling * LOG2E) - shift)
            held[pl.ds(j * BLOCK, BLOCK), :] = part
            part_total = jnp.sum(part.reshape(-1, 8, BLOCK), axis=0)
            total = part_total if total is None else total + part_total
        inverse = 1.0 / (sink_part + jnp.sum(total, axis=0, keepdims=True))
        for j in range(slots):
            weight[b, pl.ds(j * BLOCK, BLOCK), :] = (
                held[pl.ds(j * BLOCK, BLOCK), :] * inverse).astype(BF16)
        sink_weight[pl.ds(b, 1), :] = sink_part * inverse

    def step(b, top, u):
        top_next = scores_of(jnp.minimum(b + 1, blocks - 1), score.at[(u + 1) % unroll])
        attend(jnp.maximum(b - 1, 0))
        softmax(b, top, score.at[u])
        return top_next

    def several(i, top):
        for u in range(unroll):
            top = step(unroll * i + u, top, u)
        return top

    def one_chunk(i, top):
        trips = chunk // unroll
        top = lax.fori_loop(i * trips, (i + 1) * trips, several, top)
        send_weight(i).start()
        return top

    weight[0] = jnp.zeros(weight.shape[1:], BF16)
    loads[0].wait()
    top = scores_of(0, score.at[0])
    loads[1].wait()
    lax.fori_loop(0, chunks, one_chunk, top)
    attend(blocks - 1)
    send_result = pltpu.make_async_copy(result, out, result_sem)
    send_result.start()
    for i in range(chunks):
        send_weight(i).wait()
    send_result.wait()


def value_kernel(blocks, slots, per_device, links, grads_in, attended_in, weights, sink_weight, out,
                 row_dot, grads, attended, weight, value_sum, ready, load_sem, send_sem):
    tokens = grads.shape[1]
    chunks = load_sem.shape[1]
    chunk = blocks // chunks

    def fetch(i):
        peers = pl.ds(i * (chunk // per_device), chunk // per_device)
        span = pl.ds(i * chunk, chunk)
        return (
            pltpu.make_async_copy(grads_in.at[peers], grads.at[peers], load_sem.at[0, i]),
            pltpu.make_async_copy(attended_in.at[peers], attended.at[peers], load_sem.at[1, i]),
            pltpu.make_async_copy(weights.at[span], weight.at[span], load_sem.at[2, i]),
        )

    for i in range(2):
        for load in fetch(i):
            load.start()

    def prepare(c, carry):
        value_sum[c] = jnp.zeros((BLOCK, HEAD), F32)
        return carry

    lax.fori_loop(0, blocks, prepare, 0, unroll=4)

    def one_block(b):
        grad = tile(grads, b, 0, per_device)[...]
        parts = dot(weight[b], grad, NN)
        product = grad.astype(F32) * tile(attended, b, 0, per_device)[...].astype(F32)
        row_dot[pl.ds(b, 1), :] = jnp.sum(product.T, axis=0, keepdims=True)
        for j in range(slots):
            value_sum[links[b * slots + j]] += parts[j * BLOCK:(j + 1) * BLOCK]

    def one_chunk(i, carry):
        @pl.when(i + 2 < chunks)
        def _():
            for load in fetch(i + 2):
                load.start()

        for load in fetch(i):
            load.wait()
        for u in range(chunk):
            one_block(i * chunk + u)
        return carry

    lax.fori_loop(0, chunks, one_chunk, 0)

    def finish(c, carry):
        tile(ready, c, 0, per_device)[...] = value_sum[c].astype(BF16)
        return carry

    lax.fori_loop(0, blocks, finish, 0, unroll=4)
    rest = -jnp.sum(sink_weight[...] * row_dot[...], keepdims=True)
    row = lax.broadcasted_iota(jnp.int32, (EXTRA, HEAD), 0)
    stacked = jnp.zeros((EXTRA, HEAD), F32)
    for i in range(3):
        addend = rest.astype(BF16).astype(F32)
        stacked = jnp.where(row == i, addend, stacked)
        rest = rest - addend
    ready[:, pl.ds(tokens, EXTRA), :] = jnp.broadcast_to(
        stacked.astype(BF16)[None], (ready.shape[0], EXTRA, HEAD))
    send = pltpu.make_async_copy(ready, out, send_sem)
    send.start()
    send.wait()


def backward_kernel(blocks, slots, per_device, scaling, links, rows_in, grads_in, weights, row_dot,
                    out, change, key_sum, rows, grads, weight, ready, weight_sem, load_sem, send_sem):
    tokens = grads.shape[1]
    chunks = weight_sem.shape[0]
    chunk = blocks // chunks
    unroll = change.shape[0]
    values_at = pl.ds(2 * tokens, tokens)
    others_at = pl.ds(0, 2 * tokens)
    loads = [
        pltpu.make_async_copy(grads_in, grads, load_sem.at[0]),
        pltpu.make_async_copy(rows_in.at[:, values_at, :], rows.at[:, values_at, :], load_sem.at[1]),
        pltpu.make_async_copy(rows_in.at[:, others_at, :], rows.at[:, others_at, :], load_sem.at[2]),
    ]

    def fetch(i):
        span = pl.ds(i * chunk, chunk)
        return pltpu.make_async_copy(weights.at[span], weight.at[span], weight_sem.at[i])

    loads[0].start()
    loads[1].start()
    fetch(0).start()
    loads[2].start()
    fetch(1).start()

    def prepare(c, carry):
        key_sum[c] = jnp.zeros((BLOCK, HEAD), F32)
        return carry

    lax.fori_loop(0, blocks, prepare, 0, unroll=4)

    def score_grads(b, held):
        values = jnp.concatenate(
            [tile(rows, links[b * slots + j], 2, per_device)[...] for j in range(slots)], axis=0)
        grad_weight = dot(values, tile(grads, b, 0, per_device)[...], NT)
        dots = row_dot[pl.ds(b, 1), :]
        held[...] = (weight[b].astype(F32) * (grad_weight - dots)).astype(BF16)

    def collect(b, held):
        parts = dot(held[...], tile(rows, b, 0, per_device)[...], NN)
        for j in range(slots):
            key_sum[links[b * slots + j]] += parts[j * BLOCK:(j + 1) * BLOCK]

    def query_grad(b, held):
        keys = jnp.concatenate(
            [tile(rows, links[b * slots + j], 1, per_device)[...] for j in range(slots)], axis=0)
        tile(ready, b, 0, per_device)[...] = (dot(held[...], keys, TN) * scaling).astype(BF16)

    def several(i, carry):
        for u in range(unroll):
            b = unroll * i + u
            score_grads(jnp.minimum(b + 1, blocks - 1), change.at[(u + 1) % unroll])
            collect(b, change.at[u])
            query_grad(b, change.at[u])
        return carry

    for load in loads[:2]:
        load.wait()
    fetch(0).wait()
    score_grads(0, change.at[0])
    loads[2].wait()

    def one_chunk(i, carry):
        @pl.when(i + 2 < chunks)
        def _():
            fetch(i + 2).start()

        @pl.when(i + 1 < chunks)
        def _():
            fetch(i + 1).wait()

        trips = chunk // unroll
        return lax.fori_loop(i * trips, (i + 1) * trips, several, carry)

    lax.fori_loop(0, chunks, one_chunk, 0)

    def finish(c, carry):
        tile(ready, c, 1, per_device)[...] = (key_sum[c] * scaling).astype(BF16)
        return carry

    lax.fori_loop(0, blocks, finish, 0, unroll=4)
    send = pltpu.make_async_copy(ready, out, send_sem)
    send.start()
    send.wait()


def forward(links, sink, rows, scaling, slots):
    peers, depth, _ = rows.shape
    tokens = depth // 3
    per_device = tokens // BLOCK
    blocks = peers * per_device
    return pl.pallas_call(
        functools.partial(forward_kernel, blocks, slots, per_device, scaling),
        out_shape=(
            jax.ShapeDtypeStruct((peers, tokens, HEAD), BF16),
            jax.ShapeDtypeStruct((blocks, slots * BLOCK, BLOCK), BF16),
            jax.ShapeDtypeStruct((blocks, BLOCK), F32),
        ),
        in_specs=[SMEM_WHOLE, SMEM_WHOLE, IN_PLACE],
        out_specs=(IN_PLACE, IN_PLACE, VMEM_WHOLE),
        scratch_shapes=[
            pltpu.VMEM((8, slots * BLOCK, BLOCK), F32),
            pltpu.VMEM(rows.shape, BF16),
            pltpu.VMEM((blocks, slots * BLOCK, BLOCK), BF16),
            pltpu.VMEM((peers, tokens, HEAD), BF16),
            pltpu.SemaphoreType.DMA((2,)),
            pltpu.SemaphoreType.DMA((4,)),
            pltpu.SemaphoreType.DMA,
        ],
        compiler_params=pltpu.CompilerParams(vmem_limit_bytes=VMEM_GRANT),
        cost_estimate=pl.CostEstimate(
            flops=4 * blocks * slots * BLOCK * BLOCK * HEAD,
            bytes_accessed=14 << 20,
            transcendentals=blocks * slots * BLOCK * BLOCK,
        ),
        name="forward",
    )(links, sink, rows)


def value_grad(links, grads, attended, weights, sink_weight):
    peers, tokens, _ = grads.shape
    per_device = tokens // BLOCK
    blocks = peers * per_device
    slots = weights.shape[1] // BLOCK
    return pl.pallas_call(
        functools.partial(value_kernel, blocks, slots, per_device),
        out_shape=(
            jax.ShapeDtypeStruct((peers, tokens + EXTRA, HEAD), BF16),
            jax.ShapeDtypeStruct((blocks, BLOCK), F32),
        ),
        in_specs=[SMEM_WHOLE, IN_PLACE, IN_PLACE, IN_PLACE, VMEM_WHOLE],
        out_specs=(IN_PLACE, VMEM_WHOLE),
        scratch_shapes=[
            pltpu.VMEM((peers, tokens, HEAD), BF16),
            pltpu.VMEM((peers, tokens, HEAD), BF16),
            pltpu.VMEM(weights.shape, BF16),
            pltpu.VMEM((blocks, BLOCK, HEAD), F32),
            pltpu.VMEM((peers, tokens + EXTRA, HEAD), BF16),
            pltpu.SemaphoreType.DMA((3, 4)),
            pltpu.SemaphoreType.DMA,
        ],
        compiler_params=pltpu.CompilerParams(vmem_limit_bytes=VMEM_GRANT),
        cost_estimate=pl.CostEstimate(
            flops=2 * blocks * slots * BLOCK * BLOCK * HEAD,
            bytes_accessed=12 << 20,
            transcendentals=0,
        ),
        name="value_grad",
    )(links, grads, attended, weights, sink_weight)


def backward(links, rows, grads, weights, row_dot, scaling):
    peers, tokens, _ = grads.shape
    per_device = tokens // BLOCK
    blocks = peers * per_device
    slots = weights.shape[1] // BLOCK
    return pl.pallas_call(
        functools.partial(backward_kernel, blocks, slots, per_device, scaling),
        out_shape=jax.ShapeDtypeStruct((peers, 2 * tokens, HEAD), BF16),
        in_specs=[SMEM_WHOLE, IN_PLACE, IN_PLACE, IN_PLACE, VMEM_WHOLE],
        out_specs=IN_PLACE,
        scratch_shapes=[
            pltpu.VMEM((8, slots * BLOCK, BLOCK), BF16),
            pltpu.VMEM((blocks, BLOCK, HEAD), F32),
            pltpu.VMEM(rows.shape, BF16),
            pltpu.VMEM((peers, tokens, HEAD), BF16),
            pltpu.VMEM(weights.shape, BF16),
            pltpu.VMEM((peers, 2 * tokens, HEAD), BF16),
            pltpu.SemaphoreType.DMA((4,)),
            pltpu.SemaphoreType.DMA((3,)),
            pltpu.SemaphoreType.DMA,
        ],
        compiler_params=pltpu.CompilerParams(vmem_limit_bytes=VMEM_GRANT),
        cost_estimate=pl.CostEstimate(
            flops=6 * blocks * slots * BLOCK * BLOCK * HEAD,
            bytes_accessed=16 << 20,
            transcendentals=0,
        ),
        name="backward",
    )(links, rows, grads, weights, row_dot)


def pack_kernel(*refs):
    *sources, out, flat, split, load_sem, send_sem = refs
    heads, tokens = split.shape[1], split.shape[2]
    loads, sends = [], []
    for part, source in enumerate(sources):
        loads.append(pltpu.make_async_copy(source.at[0], flat.at[part], load_sem.at[part]))
        span = out.at[:, pl.ds(part * tokens, tokens), :]
        sends.append(pltpu.make_async_copy(split.at[part], span, send_sem.at[part]))
        loads[part].start()
    for part in range(len(sources)):
        loads[part].wait()
        for h in range(heads):
            split[part, h] = flat[part, :, pl.ds(h * HEAD, HEAD)]
        sends[part].start()
    for send in sends:
        send.wait()


def pack(*arrays):
    _, tokens, columns = arrays[0].shape
    heads, count = columns // HEAD, len(arrays)
    return pl.pallas_call(
        pack_kernel,
        out_shape=jax.ShapeDtypeStruct((heads, count * tokens, HEAD), arrays[0].dtype),
        in_specs=[IN_PLACE] * count,
        out_specs=IN_PLACE,
        scratch_shapes=[
            pltpu.VMEM((count, tokens, columns), arrays[0].dtype),
            pltpu.VMEM((count, heads, tokens, HEAD), arrays[0].dtype),
            pltpu.SemaphoreType.DMA((count,)),
            pltpu.SemaphoreType.DMA((count,)),
        ],
        compiler_params=pltpu.CompilerParams(vmem_limit_bytes=VMEM_GRANT),
        cost_estimate=pl.CostEstimate(
            flops=0, bytes_accessed=4 * count * tokens * columns, transcendentals=0),
        name="pack",
    )(*arrays)


def unpack_kernel(source, *refs):
    *outs, split, flat, load_sem, send_sem = refs
    heads, tokens = source.shape[0], flat.shape[1]
    loads, sends = [], []
    for part, out in enumerate(outs):
        span = source.at[:, pl.ds(part * tokens, tokens), :]
        loads.append(pltpu.make_async_copy(span, split.at[part], load_sem.at[part]))
        sends.append(pltpu.make_async_copy(flat.at[part], out.at[0], send_sem.at[part]))
        loads[part].start()
    for part in range(len(outs)):
        loads[part].wait()
        for h in range(heads):
            flat[part, :, pl.ds(h * HEAD, HEAD)] = split[part, h]
        sends[part].start()
    for send in sends:
        send.wait()


def unpack(array, tokens, count):
    heads = array.shape[0]
    return pl.pallas_call(
        unpack_kernel,
        out_shape=(jax.ShapeDtypeStruct((1, tokens, heads * HEAD), array.dtype),) * count,
        in_specs=[IN_PLACE],
        out_specs=(IN_PLACE,) * count,
        scratch_shapes=[
            pltpu.VMEM((count, heads, tokens, HEAD), array.dtype),
            pltpu.VMEM((count, tokens, heads * HEAD), array.dtype),
            pltpu.SemaphoreType.DMA((count,)),
            pltpu.SemaphoreType.DMA((count,)),
        ],
        compiler_params=pltpu.CompilerParams(vmem_limit_bytes=VMEM_GRANT),
        cost_estimate=pl.CostEstimate(
            flops=0, bytes_accessed=4 * heads * count * tokens * HEAD, transcendentals=0),
        name="unpack",
    )(array)


def exchange(array):
    return lax.all_to_all(array, "seq", split_axis=0, concat_axis=0, tiled=True)


def sum_over_documents(values):
    size = lax.axis_size("dp")
    stride = 1
    while stride < size:
        width = min(4, size // stride)
        shifted = []
        for k in range(1, width):
            pairs = []
            for i in range(size):
                digit = i // stride % width
                pairs.append((i, i + ((digit + k) % width - digit) * stride))
            shifted.append(lax.ppermute(values, "dp", pairs))
        values = functools.reduce(jnp.add, shifted, values)
        stride *= width
    return values


def on_device(query_rows, key_rows, value_rows, sink_logit, grad_out, pattern):
    heads, blocks, slots = pattern.shape
    head = lax.axis_index("seq")
    links = lax.dynamic_index_in_dim(pattern, head, 0, keepdims=False).reshape(blocks * slots)
    sink = lax.dynamic_slice_in_dim(sink_logit, head, 1, 0)
    scaling = HEAD ** -0.5

    tokens = query_rows.shape[1]
    grad_out, links, sink = lax.optimization_barrier((grad_out, links, sink))
    rows = exchange(pack(query_rows, key_rows, value_rows))
    grads = exchange(pack(grad_out))
    attended, weights, sink_weight = forward(links, sink, rows, scaling, slots)
    attended_tokens = exchange(attended)
    values, row_dot = value_grad(links, grads, attended, weights, sink_weight)
    attended_tokens, values, row_dot = lax.optimization_barrier((attended_tokens, values, row_dot))
    value_tokens = exchange(values)
    others = backward(links, rows, grads, weights, row_dot, scaling)
    value_tokens, others = lax.optimization_barrier((value_tokens, others))
    other_tokens = exchange(others)

    addends = value_tokens[:, tokens:tokens + 3, 0].astype(F32)
    grad_sink = sum_over_documents(jnp.sum(addends, axis=1)) / lax.axis_size("dp")
    (out,) = unpack(attended_tokens, tokens, 1)
    (grad_value,) = unpack(value_tokens, tokens, 1)
    grad_query, grad_key = unpack(other_tokens, tokens, 2)
    return out, grad_query, grad_key, grad_value, grad_sink


def solution(mesh):
    placed = (
        P("dp", "seq", None),
        P("dp", "seq", None),
        P("dp", "seq", None),
        P(),
        P("dp", "seq", None),
        P(),
    )
    return jax.shard_map(
        on_device,
        mesh=mesh,
        in_specs=placed,
        out_specs=(
            P("dp", "seq", None),
            P("dp", "seq", None),
            P("dp", "seq", None),
            P("dp", "seq", None),
            P(),
        ),
        check_vma=False,
    )
```

time: 168 us -> 156 us (0.929)
  waiting for transfers between devices: 64 us -> 58.4 us
  Pallas kernels: 55.8 us -> 50.7 us
  local copies, waits for them, and re-layouts: 5.02 us -> 1.34 us
  starting transfers between devices: 40.2 us -> 42.3 us
    pallas_call x1, Pallas kernels: 22.9 us -> 14.6 us  [backward(): pl.pallas_call(functools.partial(backward_kernel, blocks, slots, per_devi...]
    all_to_all x4 -> x5, waiting for transfers between devices: 62 us -> 53.9 us  [exchange(): return lax.all_to_all(array, 'seq', split_axis=0, concat_axis=0, tiled=True)]
    unnamed x10 -> x4, local copies, waits for them, and re-layouts: 3.7 us -> 0.02 us
    pallas_call x2 -> x3, Pallas kernels: 4.49 us -> 7.87 us  [unpack(): pl.pallas_call(unpack_kernel, out_shape=(jax.ShapeDtypeStruct((1, tokens,...]
    pallas_call x1, Pallas kernels: 17.9 us -> 14.6 us  [forward(): pl.pallas_call(functools.partial(forward_kernel, blocks, slots, per_devic...]
    pallas_call x1, Pallas kernels: 4.88 us -> 8.15 us  [value_grad(): pl.pallas_call(functools.partial(value_kernel, blocks, slots, per_device)...]
    ppermute x6, waiting for transfers between devices: 2.04 us -> 4.57 us  [sum_over_documents(): shifted.append(lax.ppermute(values, 'dp', pairs))]
    all_to_all x4 -> x5, starting transfers between devices: 29.4 us -> 31.4 us  [exchange(): return lax.all_to_all(array, 'seq', split_axis=0, concat_axis=0, tiled=True)]
  transfers between devices with their start and end apart: 10 -> 11, of which waited for: 4 -> 8; matrix products, arithmetic and copies ran while one was open for 2% -> 2% of each run, Pallas kernels for 27% -> 29%
where the time goes in v3:
time: 156 us; the launch traced here: 155 us
  waiting for transfers between devices  58.4 us (37%)
  Pallas kernels  50.7 us (32%)
  starting transfers between devices  42.3 us (27%)
    all_to_all x5, waiting for transfers between devices, exchange(): return lax.all_to_all(array, 'seq', split_axis=0, concat_axis=0, tiled=True)  53.9 us
    all_to_all x5, starting transfers between devices, exchange(): return lax.all_to_all(array, 'seq', split_axis=0, concat_axis=0, tiled=True)  31.4 us
    pallas_call x1, Pallas kernels, forward(): pl.pallas_call(functools.partial(forward_kernel, blocks, slots, per_devic...  14.6 us
    pallas_call x1, Pallas kernels, backward(): pl.pallas_call(functools.partial(backward_kernel, blocks, slots, per_devi...  14.6 us
    ppermute x6, starting transfers between devices, sum_over_documents(): shifted.append(lax.ppermute(values, 'dp', pairs))  10.8 us
    pallas_call x1, Pallas kernels, value_grad(): pl.pallas_call(functools.partial(value_kernel, blocks, slots, per_device)...  8.15 us
    pallas_call x3, Pallas kernels, unpack(): pl.pallas_call(unpack_kernel, out_shape=(jax.ShapeDtypeStruct((1, tokens,...  7.87 us
    pallas_call x2, Pallas kernels, pack(): pl.pallas_call(pack_kernel, out_shape=jax.ShapeDtypeStruct((heads, count...  5.55 us
  transfers between devices with their start and end apart: 11, of which 8 were waited for; matrix products, arithmetic and copies ran while one was open for 2% of the time, Pallas kernels for 29%

profile of v3, /device:TPU:64, one launch (start us, length us, event | category | flops | bytes accessed | tf_op | source)
XLA Modules:
  0.0 155.0 jit_solution(7114695100849948806)
XLA Ops:
  0.6 0.0 copy-start
  0.6 3.2 %pack.2 = bf16[16,768,128]{2,1,0:T(8,128)(2,1)} custom-call(bf16[1,256,2048]{2,1,0:T(8,128)(2,1)} %refs_0_.1, bf16[1,256,2048]{2,1,0:T(8,128)(2,1)} %refs_1_.1, bf16[1,256,2048]{2,1,0:T(8,128)(2,1)} %refs_2_.1), custom_call_target="tpu_custom_call" | custom-call | bytes 6291456 | tf_op jit(solution)/shard_map/pack/pallas_call | solution.py:385
  3.8 7.1 %all-to-all-start = ((bf16[16,768,128]{2,1,0:T(8,128)(2,1)}), bf16[16,768,128]{2,1,0:T(8,128)(2,1)}, u32[]{:S(2)}, u32[]{:S(2)}) async-start(bf16[16,768,128]{2,1,0:T(8,128)(2,1)} %pack.2), calls=%async_computation | async-start | bytes 6291456 | tf_op jit(solution)/shard_map/all_to_all | solution.py:442
  11.0 0.1 copy.11
  11.0 0.7 reshape.15.links
  11.7 0.6 dynamic_slice.8.sink
  12.3 2.4 %pack.3 = bf16[16,256,128]{2,1,0:T(8,128)(2,1)} custom-call(bf16[1,256,2048]{2,1,0:T(8,128)(2,1)} %refs_0_.2), custom_call_target="tpu_custom_call" | custom-call | bytes 2097152 | tf_op jit(solution)/shard_map/pack/pallas_call | solution.py:385
  14.7 38.8 %all-to-all-done.rows_in = bf16[16,768,128]{2,1,0:T(8,128)(2,1)} async-done(((bf16[16,768,128]{2,1,0:T(8,128)(2,1)}), bf16[16,768,128]{2,1,0:T(8,128)(2,1)}, u32[]{:S(2)}, u32[]{:S(2)}) %all-to-all-start) | async-done | bytes 3145760 | tf_op jit(solution)/shard_map/all_to_all | solution.py:442
  53.4 7.9 %all-to-all-start.2 = ((bf16[16,256,128]{2,1,0:T(8,128)(2,1)}), bf16[16,256,128]{2,1,0:T(8,128)(2,1)}, u32[]{:S(2)}, u32[]{:S(2)}) async-start(bf16[16,256,128]{2,1,0:T(8,128)(2,1)} %pack.3), calls=%async_computation.2 | async-start | bytes 2097152 | tf_op jit(solution)/shard_map/all_to_all | solution.py:442
  61.4 14.6 %forward.1 = (bf16[16,256,128]{2,1,0:T(8,128)(2,1)}, bf16[32,1024,128]{2,1,0:T(8,128)(2,1)}, f32[32,128]{1,0:T(8,128)}) custom-call(s32[256]{0:T(256)} %reshape.15.links, f32[1]{0:T(128)} %dynamic_slice.8.sink, bf16[16,768,128]{2,1,0:T(8,128)(2,1)} %all-to-all-done.rows_in), custom_call_target="tpu_custom_call" | custom-call | flops 2147483648 | bytes 14680064 | tf_op jit(solution)/shard_map/forward/pallas_call | solution.py:273
  75.9 1.2 all-to-all-done.2.grads_in
  77.1 6.1 %all-to-all-start.1 = ((bf16[16,256,128]{2,1,0:T(8,128)(2,1)}), bf16[16,256,128]{2,1,0:T(8,128)(2,1)}, u32[]{:S(2)}, u32[]{:S(2)}) async-start(bf16[16,256,128]{2,1,0:T(8,128)(2,1)} %get-tuple-element.22.attended_in), calls=%async_computation.1 | async-start | bytes 2097152 | tf_op jit(solution)/shard_map/all_to_all | solution.py:442
  83.2 8.1 %value_grad.1 = (bf16[16,272,128]{2,1,0:T(8,128)(2,1)}, f32[32,128]{1,0:T(8,128)}) custom-call(s32[256]{0:T(256)} %reshape.15.links, bf16[16,256,128]{2,1,0:T(8,128)(2,1)} %all-to-all-done.2.grads_in, bf16[16,256,128]{2,1,0:T(8,128)(2,1)} %get-tuple-element.22.attended_in, bf16[32,1024,128]{2,1,0:T(8,128)(2,1)} %get-tuple-element.24.weights, ...), custom_call_target="tpu_custom_call" | custom-call | flops 1073741824 | bytes 12582912 | tf_op jit(solution)/shard_map/value_grad/pallas_call | solution.py:306
  91.3 7.1 %all-to-all-done.1.source = bf16[16,256,128]{2,1,0:T(8,128)(2,1)} async-done(((bf16[16,256,128]{2,1,0:T(8,128)(2,1)}), bf16[16,256,128]{2,1,0:T(8,128)(2,1)}, u32[]{:S(2)}, u32[]{:S(2)}) %all-to-all-start.1) | async-done | bytes 1048608 | tf_op jit(solution)/shard_map/all_to_all | solution.py:442
  98.4 4.4 %all-to-all-start.3 = ((bf16[16,272,128]{2,1,0:T(8,128)(2,1)}), bf16[16,272,128]{2,1,0:T(8,128)(2,1)}, u32[]{:S(2)}, u32[]{:S(2)}) async-start(bf16[16,272,128]{2,1,0:T(8,128)(2,1)} %get-tuple-element.29), calls=%async_computation.3 | async-start | bytes 2228224 | tf_op jit(solution)/shard_map/all_to_all | solution.py:442
  102.8 14.6 %backward.1 = bf16[16,512,128]{2,1,0:T(8,128)(2,1)} custom-call(s32[256]{0:T(256)} %reshape.15.links, bf16[16,768,128]{2,1,0:T(8,128)(2,1)} %all-to-all-done.rows_in, bf16[16,256,128]{2,1,0:T(8,128)(2,1)} %all-to-all-done.2.grads_in, bf16[32,1024,128]{2,1,0:T(8,128)(2,1)} %get-tuple-element.24.weights, f32[32,128]{1,0:T(8,128)} %get-tuple-element.30.row_dot), custom_call_target="tpu_custom_call" | custom-call | flops 3221225472 | bytes 16777216 | tf_op jit(solution)/shard_map/backward/pallas_call | solution.py:338
  117.4 1.2 all-to-all-done.3.source
  118.5 6.0 %all-to-all-start.4 = ((bf16[16,512,128]{2,1,0:T(8,128)(2,1)}), bf16[16,512,128]{2,1,0:T(8,128)(2,1)}, u32[]{:S(2)}, u32[]{:S(2)}) async-start(bf16[16,512,128]{2,1,0:T(8,128)(2,1)} %backward.1), calls=%async_computation.4 | async-start | bytes 4194304 | tf_op jit(solution)/shard_map/all_to_all | solution.py:442
  124.5 2.5 %unpack.3 = bf16[1,256,2048]{2,1,0:T(8,128)(2,1)} custom-call(bf16[16,256,128]{2,1,0:T(8,128)(2,1)} %all-to-all-done.1.source), custom_call_target="tpu_custom_call" | custom-call | bytes 2097152 | tf_op jit(solution)/shard_map/unpack/pallas_call | solution.py:423
  127.0 2.5 %unpack.5 = bf16[1,256,2048]{2,1,0:T(8,128)(2,1)} custom-call(bf16[16,272,128]{2,1,0:T(8,128)(2,1)} %all-to-all-done.3.source), custom_call_target="tpu_custom_call" | custom-call | bytes 2097152 | tf_op jit(solution)/shard_map/unpack/pallas_call | solution.py:423
  129.6 1.0 convert_reduce_fusion
  130.5 0.1 collective-permute-start.2
  130.6 2.0 %collective-permute-start.1 = (f32[16]{0:T(128)S(1)}, f32[16]{0:T(128)S(1)}, u32[]{:S(2)}, u32[]{:S(2)}) collective-permute-start(f32[16]{0:T(128)S(1)} %convert_reduce_fusion), channel_id=1, source_target_pairs={{0,2},{1,3},{2,0},{3,1},{4,6},{5,7},{6,4},{7,5},{8,10},{9,11},{10,... | collective-permute-start | bytes 200 | tf_op jit(solution)/shard_map/ppermute | solution.py:456
  132.6 0.1 collective-permute-start
  132.8 1.5 collective-permute-done.1
  134.2 1.3 collective-permute-done
  135.6 5.9 %collective-permute-start.4 = (f32[16]{0:T(128)S(1)}, f32[16]{0:T(128)S(1)}, u32[]{:S(2)}, u32[]{:S(2)}) collective-permute-start(f32[16]{0:T(128)S(1)} %add_add_fusion), channel_id=1, source_target_pairs={{0,8},{1,9},{2,10},{3,11},{4,12},{5,13},{6,14},{7,15},{8,0},{9,1},... | collective-permute-start | bytes 200 | tf_op jit(solution)/shard_map/ppermute | solution.py:456
  141.5 2.7 %collective-permute-start.3 = (f32[16]{0:T(128)S(1)}, f32[16]{0:T(128)S(1)}, u32[]{:S(2)}, u32[]{:S(2)}) collective-permute-start(f32[16]{0:T(128)S(1)} %add_add_fusion), channel_id=1, source_target_pairs={{0,4},{1,5},{2,6},{3,7},{4,8},{5,9},{6,10},{7,11},{8,12},{9,13},{1... | collective-permute-start | bytes 200 | tf_op jit(solution)/shard_map/ppermute | solution.py:456
  144.2 1.7 %collective-permute-done.3 = f32[16]{0:T(128)S(1)} collective-permute-done((f32[16]{0:T(128)S(1)}, f32[16]{0:T(128)S(1)}, u32[]{:S(2)}, u32[]{:S(2)}) %collective-permute-start.3) | collective-permute-done | bytes 96 | tf_op jit(solution)/shard_map/ppermute | solution.py:456
  146.0 0.5 add_multiply_fusion
  146.5 5.7 %all-to-all-done.4.source = bf16[16,512,128]{2,1,0:T(8,128)(2,1)} async-done(((bf16[16,512,128]{2,1,0:T(8,128)(2,1)}), bf16[16,512,128]{2,1,0:T(8,128)(2,1)}, u32[]{:S(2)}, u32[]{:S(2)}) %all-to-all-start.4) | async-done | bytes 2097184 | tf_op jit(solution)/shard_map/all_to_all | solution.py:442
  152.2 2.9 %unpack.4 = (bf16[1,256,2048]{2,1,0:T(8,128)(2,1)}, bf16[1,256,2048]{2,1,0:T(8,128)(2,1)}) custom-call(bf16[16,512,128]{2,1,0:T(8,128)(2,1)} %all-to-all-done.4.source), custom_call_target="tpu_custom_call" | custom-call | bytes 4194304 | tf_op jit(solution)/shard_map/unpack/pallas_call | solution.py:423
  (9 shorter events, 0.0 us)
Async XLA Ops:
  0.6 10.3 %copy-start = (s32[16,32,8]{1,2,0:T(8,128)S(1)}, s32[16,32,8]{1,2,0:T(8,128)}, u32[]{:S(2)}) copy-start(s32[16,32,8]{1,2,0:T(8,128)} %param.11) | copy-start | bytes 49156
  3.8 7.9 %copy-start.1 = (f32[16]{0:T(128)S(1)}, f32[16]{0:T(128)}, u32[]{:S(2)}) copy-start(f32[16]{0:T(128)} %param.9) | copy-start | bytes 196
  3.8 49.6 %all-to-all-start = ((bf16[16,768,128]{2,1,0:T(8,128)(2,1)}), bf16[16,768,128]{2,1,0:T(8,128)(2,1)}, u32[]{:S(2)}, u32[]{:S(2)}) async-start(bf16[16,768,128]{2,1,0:T(8,128)(2,1)} %pack.2), calls=%async_computation | async-start | bytes 6291456 | tf_op jit(solution)/shard_map/all_to_all | solution.py:442
  53.4 23.7 %all-to-all-start.2 = ((bf16[16,256,128]{2,1,0:T(8,128)(2,1)}), bf16[16,256,128]{2,1,0:T(8,128)(2,1)}, u32[]{:S(2)}, u32[]{:S(2)}) async-start(bf16[16,256,128]{2,1,0:T(8,128)(2,1)} %pack.3), calls=%async_computation.2 | async-start | bytes 2097152 | tf_op jit(solution)/shard_map/all_to_all | solution.py:442
  77.1 21.3 %all-to-all-start.1 = ((bf16[16,256,128]{2,1,0:T(8,128)(2,1)}), bf16[16,256,128]{2,1,0:T(8,128)(2,1)}, u32[]{:S(2)}, u32[]{:S(2)}) async-start(bf16[16,256,128]{2,1,0:T(8,128)(2,1)} %get-tuple-element.22.attended_in), calls=%async_computation.1 | async-start | bytes 2097152 | tf_op jit(solution)/shard_map/all_to_all | solution.py:442
  98.4 20.1 %all-to-all-start.3 = ((bf16[16,272,128]{2,1,0:T(8,128)(2,1)}), bf16[16,272,128]{2,1,0:T(8,128)(2,1)}, u32[]{:S(2)}, u32[]{:S(2)}) async-start(bf16[16,272,128]{2,1,0:T(8,128)(2,1)} %get-tuple-element.29), calls=%async_computation.3 | async-start | bytes 2228224 | tf_op jit(solution)/shard_map/all_to_all | solution.py:442
  118.5 33.6 %all-to-all-start.4 = ((bf16[16,512,128]{2,1,0:T(8,128)(2,1)}), bf16[16,512,128]{2,1,0:T(8,128)(2,1)}, u32[]{:S(2)}, u32[]{:S(2)}) async-start(bf16[16,512,128]{2,1,0:T(8,128)(2,1)} %backward.1), calls=%async_computation.4 | async-start | bytes 4194304 | tf_op jit(solution)/shard_map/all_to_all | solution.py:442
  130.5 2.2 %collective-permute-start.2 = (f32[16]{0:T(128)S(1)}, f32[16]{0:T(128)S(1)}, u32[]{:S(2)}, u32[]{:S(2)}) collective-permute-start(f32[16]{0:T(128)S(1)} %convert_reduce_fusion), channel_id=1, source_target_pairs={{0,3},{1,0},{2,1},{3,2},{4,7},{5,4},{6,5},{7,6},{8,11},{9,8},{10,9... | collective-permute-start | bytes 200 | tf_op jit(solution)/shard_map/ppermute | solution.py:456
  130.6 3.6 %collective-permute-start.1 = (f32[16]{0:T(128)S(1)}, f32[16]{0:T(128)S(1)}, u32[]{:S(2)}, u32[]{:S(2)}) collective-permute-start(f32[16]{0:T(128)S(1)} %convert_reduce_fusion), channel_id=1, source_target_pairs={{0,2},{1,3},{2,0},{3,1},{4,6},{5,7},{6,4},{7,5},{8,10},{9,11},{10,... | collective-permute-start | bytes 200 | tf_op jit(solution)/shard_map/ppermute | solution.py:456
  132.6 3.0 %collective-permute-start = (f32[16]{0:T(128)S(1)}, f32[16]{0:T(128)S(1)}, u32[]{:S(2)}, u32[]{:S(2)}) collective-permute-start(f32[16]{0:T(128)S(1)} %convert_reduce_fusion), channel_id=1, source_target_pairs={{0,1},{1,2},{2,3},{3,0},{4,5},{5,6},{6,7},{7,4},{8,9},{9,10},{10,1... | collective-permute-start | bytes 200 | tf_op jit(solution)/shard_map/ppermute | solution.py:456
  135.6 8.6 %collective-permute-start.5 = (f32[16]{0:T(128)S(1)}, f32[16]{0:T(128)S(1)}, u32[]{:S(2)}, u32[]{:S(2)}) collective-permute-start(f32[16]{0:T(128)S(1)} %add_add_fusion), channel_id=1, source_target_pairs={{0,12},{1,13},{2,14},{3,15},{4,0},{5,1},{6,2},{7,3},{8,4},{9,5},{1... | collective-permute-start | bytes 200 | tf_op jit(solution)/shard_map/ppermute | solution.py:456
  135.6 8.6 %collective-permute-start.4 = (f32[16]{0:T(128)S(1)}, f32[16]{0:T(128)S(1)}, u32[]{:S(2)}, u32[]{:S(2)}) collective-permute-start(f32[16]{0:T(128)S(1)} %add_add_fusion), channel_id=1, source_target_pairs={{0,8},{1,9},{2,10},{3,11},{4,12},{5,13},{6,14},{7,15},{8,0},{9,1},... | collective-permute-start | bytes 200 | tf_op jit(solution)/shard_map/ppermute | solution.py:456
  141.5 4.4 %collective-permute-start.3 = (f32[16]{0:T(128)S(1)}, f32[16]{0:T(128)S(1)}, u32[]{:S(2)}, u32[]{:S(2)}) collective-permute-start(f32[16]{0:T(128)S(1)} %add_add_fusion), channel_id=1, source_target_pairs={{0,4},{1,5},{2,6},{3,7},{4,8},{5,9},{6,10},{7,11},{8,12},{9,13},{1... | collective-permute-start | bytes 200 | tf_op jit(solution)/shard_map/ppermute | solution.py:456

commit v4 on v3

--- a/solution.py
+++ b/solution.py
@@ -114,8 +114,9 @@
     send_result.wait()
 
 
-def value_kernel(blocks, slots, per_device, links, grads_in, attended_in, weights, sink_weight, out,
-                 row_dot, grads, attended, weight, value_sum, ready, load_sem, send_sem):
+def value_kernel(blocks, slots, per_device, links, rows_in, grads_in, attended_in, weights,
+                 sink_weight, out, changes, row_dot, grads, attended, values, weight, change,
+                 value_sum, ready, load_sem, value_sem, change_sem, send_sem):
     tokens = grads.shape[1]
     chunks = load_sem.shape[1]
     chunk = blocks // chunks
@@ -129,6 +130,13 @@
             pltpu.make_async_copy(weights.at[span], weight.at[span], load_sem.at[2, i]),
         )
 
+    def send_change(i):
+        span = pl.ds(i * chunk, chunk)
+        return pltpu.make_async_copy(change.at[span], changes.at[span], change_sem.at[i])
+
+    load_values = pltpu.make_async_copy(
+        rows_in.at[:, pl.ds(2 * tokens, tokens), :], values, value_sem)
+    load_values.start()
     for i in range(2):
         for load in fetch(i):
             load.start()
@@ -139,13 +147,20 @@
 
     lax.fori_loop(0, blocks, prepare, 0, unroll=4)
 
-    def one_block(b):
+    def dots_of(b):
+        product = tile(grads, b, 0, per_device)[...].astype(F32)
+        product = product * tile(attended, b, 0, per_device)[...].astype(F32)
+        return jnp.sum(product.T, axis=0, keepdims=True)
+
+    def one_block(b, dots):
         grad = tile(grads, b, 0, per_device)[...]
+        chosen = [links[b * slots + j] for j in range(slots)]
+        picked = jnp.concatenate([tile(values, c, 0, per_device)[...] for c in chosen], axis=0)
+        grad_weight = dot(picked, grad, NT)
         parts = dot(weight[b], grad, NN)
-        product = grad.astype(F32) * tile(attended, b, 0, per_device)[...].astype(F32)
-        row_dot[pl.ds(b, 1), :] = jnp.sum(product.T, axis=0, keepdims=True)
-        for j in range(slots):
-            value_sum[links[b * slots + j]] += parts[j * BLOCK:(j + 1) * BLOCK]
+        change[b] = (weight[b].astype(F32) * (grad_weight - dots)).astype(BF16)
+        for j, c in enumerate(chosen):
+            value_sum[c] += parts[j * BLOCK:(j + 1) * BLOCK]
 
     def one_chunk(i, carry):
         @pl.when(i + 2 < chunks)
@@ -155,10 +170,14 @@
 
         for load in fetch(i):
             load.wait()
+        dots = [dots_of(i * chunk + u) for u in range(chunk)]
         for u in range(chunk):
-            one_block(i * chunk + u)
+            row_dot[pl.ds(i * chunk + u, 1), :] = dots[u]
+            one_block(i * chunk + u, dots[u])
+        send_change(i).start()
         return carry
 
+    load_values.wait()
     lax.fori_loop(0, chunks, one_chunk, 0)
 
     def finish(c, carry):
@@ -177,31 +196,23 @@
         stacked.astype(BF16)[None], (ready.shape[0], EXTRA, HEAD))
     send = pltpu.make_async_copy(ready, out, send_sem)
     send.start()
+    for i in range(chunks):
+        send_change(i).wait()
     send.wait()
 
 
-def backward_kernel(blocks, slots, per_device, scaling, links, rows_in, grads_in, weights, row_dot,
-                    out, change, key_sum, rows, grads, weight, ready, weight_sem, load_sem, send_sem):
-    tokens = grads.shape[1]
-    chunks = weight_sem.shape[0]
+def backward_kernel(blocks, slots, per_device, scaling, links, rows_in, changes, out, key_sum, rows,
+                    change, ready, change_sem, load_sem, send_sem):
+    chunks = change_sem.shape[0]
     chunk = blocks // chunks
-    unroll = change.shape[0]
-    values_at = pl.ds(2 * tokens, tokens)
-    others_at = pl.ds(0, 2 * tokens)
-    loads = [
-        pltpu.make_async_copy(grads_in, grads, load_sem.at[0]),
-        pltpu.make_async_copy(rows_in.at[:, values_at, :], rows.at[:, values_at, :], load_sem.at[1]),
-        pltpu.make_async_copy(rows_in.at[:, others_at, :], rows.at[:, others_at, :], load_sem.at[2]),
-    ]
+    load = pltpu.make_async_copy(rows_in.at[:, pl.ds(0, rows.shape[1]), :], rows, load_sem)
+    load.start()
 
     def fetch(i):
         span = pl.ds(i * chunk, chunk)
-        return pltpu.make_async_copy(weights.at[span], weight.at[span], weight_sem.at[i])
-
-    loads[0].start()
-    loads[1].start()
+        return pltpu.make_async_copy(changes.at[span], change.at[span], change_sem.at[i])
+
     fetch(0).start()
-    loads[2].start()
     fetch(1).start()
 
     def prepare(c, carry):
@@ -210,59 +221,38 @@
 
     lax.fori_loop(0, blocks, prepare, 0, unroll=4)
 
-    def score_grads(b, held):
-        values = jnp.concatenate(
-            [tile(rows, links[b * slots + j], 2, per_device)[...] for j in range(slots)], axis=0)
-        grad_weight = dot(values, tile(grads, b, 0, per_device)[...], NT)
-        dots = row_dot[pl.ds(b, 1), :]
-        held[...] = (weight[b].astype(F32) * (grad_weight - dots)).astype(BF16)
-
-    def collect(b, held):
-        parts = dot(held[...], tile(rows, b, 0, per_device)[...], NN)
-        for j in range(slots):
-            key_sum[links[b * slots + j]] += parts[j * BLOCK:(j + 1) * BLOCK]
-
-    def query_grad(b, held):
-        keys = jnp.concatenate(
-            [tile(rows, links[b * slots + j], 1, per_device)[...] for j in range(slots)], axis=0)
-        tile(ready, b, 0, per_device)[...] = (dot(held[...], keys, TN) * scaling).astype(BF16)
-
-    def several(i, carry):
-        for u in range(unroll):
-            b = unroll * i + u
-            score_grads(jnp.minimum(b + 1, blocks - 1), change.at[(u + 1) % unroll])
-            collect(b, change.at[u])
-            query_grad(b, change.at[u])
-        return carry
-
-    for load in loads[:2]:
-        load.wait()
-    fetch(0).wait()
-    score_grads(0, change.at[0])
-    loads[2].wait()
+    def one_block(b):
+        chosen = [links[b * slots + j] for j in range(slots)]
+        parts = dot(change[b], tile(rows, b, 0, per_device)[...], NN)
+        keys = jnp.concatenate([tile(rows, c, 1, per_device)[...] for c in chosen], axis=0)
+        tile(ready, b, 0, per_device)[...] = (dot(change[b], keys, TN) * scaling).astype(BF16)
+        for j, c in enumerate(chosen):
+            key_sum[c] += parts[j * BLOCK:(j + 1) * BLOCK]
 
     def one_chunk(i, carry):
         @pl.when(i + 2 < chunks)
         def _():
             fetch(i + 2).start()
 
-        @pl.when(i + 1 < chunks)
-        def _():
-            fetch(i + 1).wait()
-
-        trips = chunk // unroll
-        return lax.fori_loop(i * trips, (i + 1) * trips, several, carry)
-
+        fetch(i).wait()
+        for u in range(chunk):
+            one_block(i * chunk + u)
+        return carry
+
+    load.wait()
     lax.fori_loop(0, chunks, one_chunk, 0)
 
-    def finish(c, carry):
-        tile(ready, c, 1, per_device)[...] = (key_sum[c] * scaling).astype(BF16)
-        return carry
-
-    lax.fori_loop(0, blocks, finish, 0, unroll=4)
-    send = pltpu.make_async_copy(ready, out, send_sem)
-    send.start()
-    send.wait()
+    pieces = send_sem.shape[0]
+    sends = []
+    for i in range(pieces):
+        for c in range(i * blocks // pieces, (i + 1) * blocks // pieces):
+            tile(ready, c, 1, per_device)[...] = (key_sum[c] * scaling).astype(BF16)
+        peers = out.shape[0] // pieces
+        span = pl.ds(i * peers, peers)
+        sends.append(pltpu.make_async_copy(ready.at[span], out.at[span], send_sem.at[i]))
+        sends[i].start()
+    for send in sends:
+        send.wait()
 
 
 def forward(links, sink, rows, scaling, slots):
@@ -298,7 +288,7 @@
     )(links, sink, rows)
 
 
-def value_grad(links, grads, attended, weights, sink_weight):
+def value_grad(links, rows, grads, attended, weights, sink_weight):
     peers, tokens, _ = grads.shape
     per_device = tokens // BLOCK
     blocks = peers * per_device
@@ -307,58 +297,62 @@
         functools.partial(value_kernel, blocks, slots, per_device),
         out_shape=(
             jax.ShapeDtypeStruct((peers, tokens + EXTRA, HEAD), BF16),
-            jax.ShapeDtypeStruct((blocks, BLOCK), F32),
+            jax.ShapeDtypeStruct(weights.shape, BF16),
         ),
-        in_specs=[SMEM_WHOLE, IN_PLACE, IN_PLACE, IN_PLACE, VMEM_WHOLE],
-        out_specs=(IN_PLACE, VMEM_WHOLE),
+        in_specs=[SMEM_WHOLE] + [IN_PLACE] * 4 + [VMEM_WHOLE],
+        out_specs=(IN_PLACE, IN_PLACE),
         scratch_shapes=[
+            pltpu.VMEM((blocks, BLOCK), F32),
             pltpu.VMEM((peers, tokens, HEAD), BF16),
             pltpu.VMEM((peers, tokens, HEAD), BF16),
+            pltpu.VMEM((peers, tokens, HEAD), BF16),
+            pltpu.VMEM(weights.shape, BF16),
             pltpu.VMEM(weights.shape, BF16),
             pltpu.VMEM((blocks, BLOCK, HEAD), F32),
             pltpu.VMEM((peers, tokens + EXTRA, HEAD), BF16),
             pltpu.SemaphoreType.DMA((3, 4)),
             pltpu.SemaphoreType.DMA,
-        ],
-        compiler_params=pltpu.CompilerParams(vmem_limit_bytes=VMEM_GRANT),
-        cost_estimate=pl.CostEstimate(
-            flops=2 * blocks * slots * BLOCK * BLOCK * HEAD,
-            bytes_accessed=12 << 20,
-            transcendentals=0,
-        ),
-        name="value_grad",
-    )(links, grads, attended, weights, sink_weight)
-
-
-def backward(links, rows, grads, weights, row_dot, scaling):
-    peers, tokens, _ = grads.shape
-    per_device = tokens // BLOCK
-    blocks = peers * per_device
-    slots = weights.shape[1] // BLOCK
-    return pl.pallas_call(
-        functools.partial(backward_kernel, blocks, slots, per_device, scaling),
-        out_shape=jax.ShapeDtypeStruct((peers, 2 * tokens, HEAD), BF16),
-        in_specs=[SMEM_WHOLE, IN_PLACE, IN_PLACE, IN_PLACE, VMEM_WHOLE],
-        out_specs=IN_PLACE,
-        scratch_shapes=[
-            pltpu.VMEM((8, slots * BLOCK, BLOCK), BF16),
-            pltpu.VMEM((blocks, BLOCK, HEAD), F32),
-            pltpu.VMEM(rows.shape, BF16),
-            pltpu.VMEM((peers, tokens, HEAD), BF16),
-            pltpu.VMEM(weights.shape, BF16),
-            pltpu.VMEM((peers, 2 * tokens, HEAD), BF16),
             pltpu.SemaphoreType.DMA((4,)),
-            pltpu.SemaphoreType.DMA((3,)),
             pltpu.SemaphoreType.DMA,
         ],
         compiler_params=pltpu.CompilerParams(vmem_limit_bytes=VMEM_GRANT),
         cost_estimate=pl.CostEstimate(
-            flops=6 * blocks * slots * BLOCK * BLOCK * HEAD,
-            bytes_accessed=16 << 20,
+            flops=4 * blocks * slots * BLOCK * BLOCK * HEAD,
+            bytes_accessed=20 << 20,
+            transcendentals=0,
+        ),
+        name="value_grad",
+    )(links, rows, grads, attended, weights, sink_weight)
+
+
+def backward(links, rows, changes, scaling):
+    peers, depth, _ = rows.shape
+    tokens = depth // 3
+    per_device = tokens // BLOCK
+    blocks = peers * per_device
+    slots = changes.shape[1] // BLOCK
+    return pl.pallas_call(
+        functools.partial(backward_kernel, blocks, slots, per_device, scaling),
+        out_shape=jax.ShapeDtypeStruct((peers, 2 * tokens, HEAD), BF16),
+        in_specs=[SMEM_WHOLE, IN_PLACE, IN_PLACE],
+        out_specs=IN_PLACE,
+        scratch_shapes=[
+            pltpu.VMEM((blocks, BLOCK, HEAD), F32),
+            pltpu.VMEM((peers, 2 * tokens, HEAD), BF16),
+            pltpu.VMEM(changes.shape, BF16),
+            pltpu.VMEM((peers, 2 * tokens, HEAD), BF16),
+            pltpu.SemaphoreType.DMA((4,)),
+            pltpu.SemaphoreType.DMA,
+            pltpu.SemaphoreType.DMA((4,)),
+        ],
+        compiler_params=pltpu.CompilerParams(vmem_limit_bytes=VMEM_GRANT),
+        cost_estimate=pl.CostEstimate(
+            flops=4 * blocks * slots * BLOCK * BLOCK * HEAD,
+            bytes_accessed=12 << 20,
             transcendentals=0,
         ),
         name="backward",
-    )(links, rows, grads, weights, row_dot)
+    )(links, rows, changes)
 
 
 def pack_kernel(*refs):
@@ -431,10 +425,41 @@
             pltpu.SemaphoreType.DMA((count,)),
             pltpu.SemaphoreType.DMA((count,)),
         ],
-        compiler_params=pltpu.CompilerParams(vmem_limit_bytes=VMEM_GRANT),
+        compiler_params=pltpu.CompilerParams(vmem_limit_bytes=56 << 20),
         cost_estimate=pl.CostEstimate(
             flops=0, bytes_accessed=4 * heads * count * tokens * HEAD, transcendentals=0),
         name="unpack",
+    )(array)
+
+
+def unpack_last_kernel(source, *refs):
+    *outs, flat, send_sem = refs
+    heads, tokens = source.shape[0], flat.shape[1]
+    sends = []
+    for part, out in enumerate(outs):
+        for h in range(heads):
+            flat[part, :, pl.ds(h * HEAD, HEAD)] = source[h, pl.ds(part * tokens, tokens), :]
+        sends.append(pltpu.make_async_copy(flat.at[part], out.at[0], send_sem.at[part]))
+        sends[part].start()
+    for send in sends:
+        send.wait()
+
+
+def unpack_last(array, tokens, count):
+    heads = array.shape[0]
+    return pl.pallas_call(
+        unpack_last_kernel,
+        out_shape=(jax.ShapeDtypeStruct((1, tokens, heads * HEAD), array.dtype),) * count,
+        in_specs=[VMEM_WHOLE],
+        out_specs=(IN_PLACE,) * count,
+        scratch_shapes=[
+            pltpu.VMEM((count, tokens, heads * HEAD), array.dtype),
+            pltpu.SemaphoreType.DMA((count,)),
+        ],
+        compiler_params=pltpu.CompilerParams(vmem_limit_bytes=8 << 20),
+        cost_estimate=pl.CostEstimate(
+            flops=0, bytes_accessed=4 * heads * count * tokens * HEAD, transcendentals=0),
+        name="unpack_last",
     )(array)
 
 
@@ -472,10 +497,10 @@
     grads = exchange(pack(grad_out))
     attended, weights, sink_weight = forward(links, sink, rows, scaling, slots)
     attended_tokens = exchange(attended)
-    values, row_dot = value_grad(links, grads, attended, weights, sink_weight)
-    attended_tokens, values, row_dot = lax.optimization_barrier((attended_tokens, values, row_dot))
+    values, changes = value_grad(links, rows, grads, attended, weights, sink_weight)
+    attended_tokens, values, changes = lax.optimization_barrier((attended_tokens, values, changes))
     value_tokens = exchange(values)
-    others = backward(links, rows, grads, weights, row_dot, scaling)
+    others = backward(links, rows, changes, scaling)
     value_tokens, others = lax.optimization_barrier((value_tokens, others))
     other_tokens = exchange(others)
 
@@ -483,7 +508,7 @@
     grad_sink = sum_over_documents(jnp.sum(addends, axis=1)) / lax.axis_size("dp")
     (out,) = unpack(attended_tokens, tokens, 1)
     (grad_value,) = unpack(value_tokens, tokens, 1)
-    grad_query, grad_key = unpack(other_tokens, tokens, 2)
+    grad_query, grad_key = unpack_last(other_tokens, tokens, 2)
     return out, grad_query, grad_key, grad_value, grad_sink
 
 

time: 156 us -> 153 us (0.981)
  Pallas kernels: 50.7 us -> 46.9 us
  waiting for transfers between devices: 58.4 us -> 61.8 us
  starting transfers between devices: 42.3 us -> 40.1 us
    pallas_call x1, Pallas kernels: 14.6 us -> 9.52 us  [backward(): pl.pallas_call(functools.partial(backward_kernel, blocks, slots, per_devi...]
    all_to_all x5, waiting for transfers between devices: 53.9 us -> 58.2 us  [exchange(): return lax.all_to_all(array, 'seq', split_axis=0, concat_axis=0, tiled=True)]
    pallas_call x3 -> x2, Pallas kernels: 7.87 us -> 5 us  [unpack(): pl.pallas_call(unpack_kernel, out_shape=(jax.ShapeDtypeStruct((1, tokens,...]
    pallas_call x1, Pallas kernels: 8.15 us -> 10.6 us  [value_grad(): pl.pallas_call(functools.partial(value_kernel, blocks, slots, per_device)...]
    all_to_all x5, starting transfers between devices: 31.4 us -> 29.2 us  [exchange(): return lax.all_to_all(array, 'seq', split_axis=0, concat_axis=0, tiled=True)]
    pallas_call x0 -> x1, Pallas kernels: none -> 1.62 us  [unpack_last(): pl.pallas_call(unpack_last_kernel, out_shape=(jax.ShapeDtypeStruct((1, to...]
  transfers between devices with their start and end apart: 11 -> 11, of which waited for: 8 -> 6; matrix products, arithmetic and copies ran while one was open for 2% -> 2% of each run, Pallas kernels for 29% -> 28%
where the time goes in v4:
time: 153 us; the launch traced here: 152 us
  waiting for transfers between devices  61.8 us (40%)
  Pallas kernels  46.9 us (31%)
  starting transfers between devices  40.1 us (26%)
    all_to_all x5, waiting for transfers between devices, exchange(): return lax.all_to_all(array, 'seq', split_axis=0, concat_axis=0, tiled=True)  58.2 us
    all_to_all x5, starting transfers between devices, exchange(): return lax.all_to_all(array, 'seq', split_axis=0, concat_axis=0, tiled=True)  29.2 us
    pallas_call x1, Pallas kernels, forward(): pl.pallas_call(functools.partial(forward_kernel, blocks, slots, per_devic...  14.6 us
    ppermute x6, starting transfers between devices, sum_over_documents(): shifted.append(lax.ppermute(values, 'dp', pairs))  10.9 us
    pallas_call x1, Pallas kernels, value_grad(): pl.pallas_call(functools.partial(value_kernel, blocks, slots, per_device)...  10.6 us
    pallas_call x1, Pallas kernels, backward(): pl.pallas_call(functools.partial(backward_kernel, blocks, slots, per_devi...  9.52 us
    pallas_call x2, Pallas kernels, pack(): pl.pallas_call(pack_kernel, out_shape=jax.ShapeDtypeStruct((heads, count...  5.55 us
    pallas_call x2, Pallas kernels, unpack(): pl.pallas_call(unpack_kernel, out_shape=(jax.ShapeDtypeStruct((1, tokens,...  5 us
  transfers between devices with their start and end apart: 11, of which 6 were waited for; matrix products, arithmetic and copies ran while one was open for 2% of the time, Pallas kernels for 28%

profile of v4, /device:TPU:64, one launch (start us, length us, event | category | flops | bytes accessed | tf_op | source)
XLA Modules:
  0.0 152.4 jit_solution(3794756326841821333)
XLA Ops:
  0.6 0.0 copy-start
  0.6 3.2 %pack.2 = bf16[16,768,128]{2,1,0:T(8,128)(2,1)} custom-call(bf16[1,256,2048]{2,1,0:T(8,128)(2,1)} %refs_0_.1, bf16[1,256,2048]{2,1,0:T(8,128)(2,1)} %refs_1_.1, bf16[1,256,2048]{2,1,0:T(8,128)(2,1)} %refs_2_.1), custom_call_target="tpu_custom_call" | custom-call | bytes 6291456 | tf_op jit(solution)/shard_map/pack/pallas_call | solution.py:379
  3.8 0.0 copy-start.1
  3.8 7.1 %all-to-all-start = ((bf16[16,768,128]{2,1,0:T(8,128)(2,1)}), bf16[16,768,128]{2,1,0:T(8,128)(2,1)}, u32[]{:S(2)}, u32[]{:S(2)}) async-start(bf16[16,768,128]{2,1,0:T(8,128)(2,1)} %pack.2), calls=%async_computation | async-start | bytes 6291456 | tf_op jit(solution)/shard_map/all_to_all | solution.py:467
  11.0 0.1 copy.11
  11.0 0.7 reshape.15.links
  11.7 0.6 dynamic_slice.8.sink
  12.3 2.4 %pack.3 = bf16[16,256,128]{2,1,0:T(8,128)(2,1)} custom-call(bf16[1,256,2048]{2,1,0:T(8,128)(2,1)} %refs_0_.2), custom_call_target="tpu_custom_call" | custom-call | bytes 2097152 | tf_op jit(solution)/shard_map/pack/pallas_call | solution.py:379
  14.7 38.8 %all-to-all-done.rows_in = bf16[16,768,128]{2,1,0:T(8,128)(2,1)} async-done(((bf16[16,768,128]{2,1,0:T(8,128)(2,1)}), bf16[16,768,128]{2,1,0:T(8,128)(2,1)}, u32[]{:S(2)}, u32[]{:S(2)}) %all-to-all-start) | async-done | bytes 3145760 | tf_op jit(solution)/shard_map/all_to_all | solution.py:467
  53.4 7.9 %all-to-all-start.2 = ((bf16[16,256,128]{2,1,0:T(8,128)(2,1)}), bf16[16,256,128]{2,1,0:T(8,128)(2,1)}, u32[]{:S(2)}, u32[]{:S(2)}) async-start(bf16[16,256,128]{2,1,0:T(8,128)(2,1)} %pack.3), calls=%async_computation.2 | async-start | bytes 2097152 | tf_op jit(solution)/shard_map/all_to_all | solution.py:467
  61.4 14.6 %forward.1 = (bf16[16,256,128]{2,1,0:T(8,128)(2,1)}, bf16[32,1024,128]{2,1,0:T(8,128)(2,1)}, f32[32,128]{1,0:T(8,128)}) custom-call(s32[256]{0:T(256)} %reshape.15.links, f32[1]{0:T(128)} %dynamic_slice.8.sink, bf16[16,768,128]{2,1,0:T(8,128)(2,1)} %all-to-all-done.rows_in), custom_call_target="tpu_custom_call" | custom-call | flops 2147483648 | bytes 14680064 | tf_op jit(solution)/shard_map/forward/pallas_call | solution.py:263
  75.9 1.2 all-to-all-done.2.grads_in
  77.1 6.1 %all-to-all-start.1 = ((bf16[16,256,128]{2,1,0:T(8,128)(2,1)}), bf16[16,256,128]{2,1,0:T(8,128)(2,1)}, u32[]{:S(2)}, u32[]{:S(2)}) async-start(bf16[16,256,128]{2,1,0:T(8,128)(2,1)} %get-tuple-element.22.attended_in), calls=%async_computation.1 | async-start | bytes 2097152 | tf_op jit(solution)/shard_map/all_to_all | solution.py:467
  83.2 10.6 %value_grad.1 = (bf16[16,272,128]{2,1,0:T(8,128)(2,1)}, bf16[32,1024,128]{2,1,0:T(8,128)(2,1)}) custom-call(s32[256]{0:T(256)} %reshape.15.links, bf16[16,768,128]{2,1,0:T(8,128)(2,1)} %all-to-all-done.rows_in, bf16[16,256,128]{2,1,0:T(8,128)(2,1)} %all-to-all-done.2.grads_in, bf16[16,256,128]{2,1,0:T(8,128)(2,1)} %get-tuple-element.22.attended_in, ...), custom_call_target="tpu_custom_call" | custom-call | flops 2147483648 | bytes 20971520 | tf_op jit(solution)/shard_map/value_grad/pallas_call | solution.py:296
  93.8 4.6 %all-to-all-done.1.source = bf16[16,256,128]{2,1,0:T(8,128)(2,1)} async-done(((bf16[16,256,128]{2,1,0:T(8,128)(2,1)}), bf16[16,256,128]{2,1,0:T(8,128)(2,1)}, u32[]{:S(2)}, u32[]{:S(2)}) %all-to-all-start.1) | async-done | bytes 1048608 | tf_op jit(solution)/shard_map/all_to_all | solution.py:467
  98.4 4.4 %all-to-all-start.3 = ((bf16[16,272,128]{2,1,0:T(8,128)(2,1)}), bf16[16,272,128]{2,1,0:T(8,128)(2,1)}, u32[]{:S(2)}, u32[]{:S(2)}) async-start(bf16[16,272,128]{2,1,0:T(8,128)(2,1)} %get-tuple-element.29), calls=%async_computation.3 | async-start | bytes 2228224 | tf_op jit(solution)/shard_map/all_to_all | solution.py:467
  102.8 9.5 %backward.1 = bf16[16,512,128]{2,1,0:T(8,128)(2,1)} custom-call(s32[256]{0:T(256)} %reshape.15.links, bf16[16,768,128]{2,1,0:T(8,128)(2,1)} %all-to-all-done.rows_in, bf16[32,1024,128]{2,1,0:T(8,128)(2,1)} %get-tuple-element.30.changes), custom_call_target="tpu_custom_call" | custom-call | flops 2147483648 | bytes 12582912 | tf_op jit(solution)/shard_map/backward/pallas_call | solution.py:334
  112.3 6.2 %all-to-all-done.3.source = bf16[16,272,128]{2,1,0:T(8,128)(2,1)} async-done(((bf16[16,272,128]{2,1,0:T(8,128)(2,1)}), bf16[16,272,128]{2,1,0:T(8,128)(2,1)}, u32[]{:S(2)}, u32[]{:S(2)}) %all-to-all-start.3) | async-done | bytes 1114144 | tf_op jit(solution)/shard_map/all_to_all | solution.py:467
  118.5 3.7 %all-to-all-start.4 = ((bf16[16,512,128]{2,1,0:T(8,128)(2,1)}), bf16[16,512,128]{2,1,0:T(8,128)(2,1)S(1)}, u32[]{:S(2)}, u32[]{:S(2)}) async-start(bf16[16,512,128]{2,1,0:T(8,128)(2,1)} %backward.1), calls=%async_computation.4 | async-start | bytes 4194304 | tf_op jit(solution)/shard_map/all_to_all | solution.py:467
  122.3 2.5 %unpack.2 = bf16[1,256,2048]{2,1,0:T(8,128)(2,1)} custom-call(bf16[16,256,128]{2,1,0:T(8,128)(2,1)} %all-to-all-done.1.source), custom_call_target="tpu_custom_call" | custom-call | bytes 2097152 | tf_op jit(solution)/shard_map/unpack/pallas_call | solution.py:417
  124.8 1.0 convert_reduce_fusion
  125.7 0.1 collective-permute-start
  125.8 2.0 %collective-permute-start.1 = (f32[16]{0:T(128)S(1)}, f32[16]{0:T(128)S(1)}, u32[]{:S(2)}, u32[]{:S(2)}) collective-permute-start(f32[16]{0:T(128)S(1)} %convert_reduce_fusion), channel_id=1, source_target_pairs={{0,2},{1,3},{2,0},{3,1},{4,6},{5,7},{6,4},{7,5},{8,10},{9,11},{10,... | collective-permute-start | bytes 200 | tf_op jit(solution)/shard_map/ppermute | solution.py:481
  127.8 1.4 collective-permute-start.2
  129.2 2.5 %unpack.3 = bf16[1,256,2048]{2,1,0:T(8,128)(2,1)} custom-call(bf16[16,272,128]{2,1,0:T(8,128)(2,1)} %all-to-all-done.3.source), custom_call_target="tpu_custom_call" | custom-call | bytes 2097152 | tf_op jit(solution)/shard_map/unpack/pallas_call | solution.py:417
  131.7 3.7 %collective-permute-start.3 = (f32[16]{0:T(128)S(1)}, f32[16]{0:T(128)S(1)}, u32[]{:S(2)}, u32[]{:S(2)}) collective-permute-start(f32[16]{0:T(128)S(1)} %add_add_fusion), channel_id=1, source_target_pairs={{0,4},{1,5},{2,6},{3,7},{4,8},{5,9},{6,10},{7,11},{8,12},{9,13},{1... | collective-permute-start | bytes 200 | tf_op jit(solution)/shard_map/ppermute | solution.py:481
  135.4 1.0 collective-permute-start.4
  136.4 2.8 %collective-permute-start.5 = (f32[16]{0:T(128)S(1)}, f32[16]{0:T(128)S(1)}, u32[]{:S(2)}, u32[]{:S(2)}) collective-permute-start(f32[16]{0:T(128)S(1)} %add_add_fusion), channel_id=1, source_target_pairs={{0,12},{1,13},{2,14},{3,15},{4,0},{5,1},{6,2},{7,3},{8,4},{9,5},{1... | collective-permute-start | bytes 200 | tf_op jit(solution)/shard_map/ppermute | solution.py:481
  139.2 3.6 %collective-permute-done.4 = f32[16]{0:T(128)S(1)} collective-permute-done((f32[16]{0:T(128)S(1)}, f32[16]{0:T(128)S(1)}, u32[]{:S(2)}, u32[]{:S(2)}) %collective-permute-start.4) | collective-permute-done | bytes 96 | tf_op jit(solution)/shard_map/ppermute | solution.py:481
  142.8 0.5 add_multiply_fusion
  143.4 7.4 %all-to-all-done.4.source = bf16[16,512,128]{2,1,0:T(8,128)(2,1)S(1)} async-done(((bf16[16,512,128]{2,1,0:T(8,128)(2,1)}), bf16[16,512,128]{2,1,0:T(8,128)(2,1)S(1)}, u32[]{:S(2)}, u32[]{:S(2)}) %all-to-all-start.4) | async-done | bytes 2097184 | tf_op jit(solution)/shard_map/all_to_all | solution.py:467
  150.8 1.6 %unpack_last.1 = (bf16[1,256,2048]{2,1,0:T(8,128)(2,1)}, bf16[1,256,2048]{2,1,0:T(8,128)(2,1)}) custom-call(bf16[16,512,128]{2,1,0:T(8,128)(2,1)S(1)} %all-to-all-done.4.source), custom_call_target="tpu_custom_call" | custom-call | bytes 4194304 | tf_op jit(solution)/shard_map/unpack_last/pallas_call | solution.py:450
  (9 shorter events, 0.0 us)
Async XLA Ops:
  0.6 10.3 %copy-start = (s32[16,32,8]{1,2,0:T(8,128)S(1)}, s32[16,32,8]{1,2,0:T(8,128)}, u32[]{:S(2)}) copy-start(s32[16,32,8]{1,2,0:T(8,128)} %param.11) | copy-start | bytes 49156
  3.8 7.9 %copy-start.1 = (f32[16]{0:T(128)S(1)}, f32[16]{0:T(128)}, u32[]{:S(2)}) copy-start(f32[16]{0:T(128)} %param.9) | copy-start | bytes 196
  3.8 49.6 %all-to-all-start = ((bf16[16,768,128]{2,1,0:T(8,128)(2,1)}), bf16[16,768,128]{2,1,0:T(8,128)(2,1)}, u32[]{:S(2)}, u32[]{:S(2)}) async-start(bf16[16,768,128]{2,1,0:T(8,128)(2,1)} %pack.2), calls=%async_computation | async-start | bytes 6291456 | tf_op jit(solution)/shard_map/all_to_all | solution.py:467
  53.4 23.7 %all-to-all-start.2 = ((bf16[16,256,128]{2,1,0:T(8,128)(2,1)}), bf16[16,256,128]{2,1,0:T(8,128)(2,1)}, u32[]{:S(2)}, u32[]{:S(2)}) async-start(bf16[16,256,128]{2,1,0:T(8,128)(2,1)} %pack.3), calls=%async_computation.2 | async-start | bytes 2097152 | tf_op jit(solution)/shard_map/all_to_all | solution.py:467
  77.1 21.3 %all-to-all-start.1 = ((bf16[16,256,128]{2,1,0:T(8,128)(2,1)}), bf16[16,256,128]{2,1,0:T(8,128)(2,1)}, u32[]{:S(2)}, u32[]{:S(2)}) async-start(bf16[16,256,128]{2,1,0:T(8,128)(2,1)} %get-tuple-element.22.attended_in), calls=%async_computation.1 | async-start | bytes 2097152 | tf_op jit(solution)/shard_map/all_to_all | solution.py:467
  98.4 20.1 %all-to-all-start.3 = ((bf16[16,272,128]{2,1,0:T(8,128)(2,1)}), bf16[16,272,128]{2,1,0:T(8,128)(2,1)}, u32[]{:S(2)}, u32[]{:S(2)}) async-start(bf16[16,272,128]{2,1,0:T(8,128)(2,1)} %get-tuple-element.29), calls=%async_computation.3 | async-start | bytes 2228224 | tf_op jit(solution)/shard_map/all_to_all | solution.py:467
  118.5 32.2 %all-to-all-start.4 = ((bf16[16,512,128]{2,1,0:T(8,128)(2,1)}), bf16[16,512,128]{2,1,0:T(8,128)(2,1)S(1)}, u32[]{:S(2)}, u32[]{:S(2)}) async-start(bf16[16,512,128]{2,1,0:T(8,128)(2,1)} %backward.1), calls=%async_computation.4 | async-start | bytes 4194304 | tf_op jit(solution)/shard_map/all_to_all | solution.py:467
  125.7 6.0 %collective-permute-start = (f32[16]{0:T(128)S(1)}, f32[16]{0:T(128)S(1)}, u32[]{:S(2)}, u32[]{:S(2)}) collective-permute-start(f32[16]{0:T(128)S(1)} %convert_reduce_fusion), channel_id=1, source_target_pairs={{0,1},{1,2},{2,3},{3,0},{4,5},{5,6},{6,7},{7,4},{8,9},{9,10},{10,1... | collective-permute-start | bytes 200 | tf_op jit(solution)/shard_map/ppermute | solution.py:481
  125.8 5.9 %collective-permute-start.1 = (f32[16]{0:T(128)S(1)}, f32[16]{0:T(128)S(1)}, u32[]{:S(2)}, u32[]{:S(2)}) collective-permute-start(f32[16]{0:T(128)S(1)} %convert_reduce_fusion), channel_id=1, source_target_pairs={{0,2},{1,3},{2,0},{3,1},{4,6},{5,7},{6,4},{7,5},{8,10},{9,11},{10,... | collective-permute-start | bytes 200 | tf_op jit(solution)/shard_map/ppermute | solution.py:481
  127.8 3.9 %collective-permute-start.2 = (f32[16]{0:T(128)S(1)}, f32[16]{0:T(128)S(1)}, u32[]{:S(2)}, u32[]{:S(2)}) collective-permute-start(f32[16]{0:T(128)S(1)} %convert_reduce_fusion), channel_id=1, source_target_pairs={{0,3},{1,0},{2,1},{3,2},{4,7},{5,4},{6,5},{7,6},{8,11},{9,8},{10,9... | collective-permute-start | bytes 200 | tf_op jit(solution)/shard_map/ppermute | solution.py:481
  131.7 7.5 %collective-permute-start.3 = (f32[16]{0:T(128)S(1)}, f32[16]{0:T(128)S(1)}, u32[]{:S(2)}, u32[]{:S(2)}) collective-permute-start(f32[16]{0:T(128)S(1)} %add_add_fusion), channel_id=1, source_target_pairs={{0,4},{1,5},{2,6},{3,7},{4,8},{5,9},{6,10},{7,11},{8,12},{9,13},{1... | collective-permute-start | bytes 200 | tf_op jit(solution)/shard_map/ppermute | solution.py:481
  135.4 7.4 %collective-permute-start.4 = (f32[16]{0:T(128)S(1)}, f32[16]{0:T(128)S(1)}, u32[]{:S(2)}, u32[]{:S(2)}) collective-permute-start(f32[16]{0:T(128)S(1)} %add_add_fusion), channel_id=1, source_target_pairs={{0,8},{1,9},{2,10},{3,11},{4,12},{5,13},{6,14},{7,15},{8,0},{9,1},... | collective-permute-start | bytes 200 | tf_op jit(solution)/shard_map/ppermute | solution.py:481
  136.4 6.4 %collective-permute-start.5 = (f32[16]{0:T(128)S(1)}, f32[16]{0:T(128)S(1)}, u32[]{:S(2)}, u32[]{:S(2)}) collective-permute-start(f32[16]{0:T(128)S(1)} %add_add_fusion), channel_id=1, source_target_pairs={{0,12},{1,13},{2,14},{3,15},{4,0},{5,1},{6,2},{7,3},{8,4},{9,5},{1... | collective-permute-start | bytes 200 | tf_op jit(solution)/shard_map/ppermute | solution.py:481
